TPU v7x, 512 devices: a whole 4x8x8 slice. The times are simulated.
512 devices in a mesh: space: 64 (over x, y, core), load: 8 (over z).
Axes of the slice: x: 4, y: 8, z: 8, core: 2. Of those that a mesh axis runs over, the one named last changes fastest.
Arguments:
- forward_disp: float32 [8, 3, 128, 128, 128], P('load', None, 'space'), may hold values from -6 to 6
- adjoint_rhs: float32 [8, 3, 128, 128, 128], P('load', None, 'space'), may hold values from -72 to 72
- modulus_factor: float32 [128, 128, 128], P('space'), may hold values from 0.5 to 2
- zone_base: float32 [8], replicated, may hold values from 0.3 to 3
- zone_ids: int32 [128, 128, 128], P('space'), may hold values from 0 to 7
- fixed_mask: int32 [128, 128, 128], P('space'), may hold values 0 or 1
Outputs:
- adjoint_disp: float32 [8, 3, 128, 128, 128], P('load', None, 'space')
- modulus_grad: float32 [128, 128, 128], P('space', 'load')
All inputs are finite; a program needn't handle non-finite values. No bound on the sum of `fixed_mask` on one device may be relied on, other than what follows from the above.
Results may differ from a plain program's by a relative error of at most 0.00016.
Values sent between devices are 32-bit elements; how exact they have to be, the bound alone decides.
A program may use at most 64 MiB of HBM per device.

v0:
```python
import jax
import jax.numpy as jnp
import numpy as np
from jax import lax
from jax.sharding import PartitionSpec as P

ITERS = 2


def from_behind(shard, axis, by):
    devices = lax.axis_size(axis)
    pairs = [(i, i + by) for i in range(devices) if 0 <= i + by < devices]
    return lax.ppermute(shard, axis, pairs)


def from_everyone(shard, axis):
    devices = lax.axis_size(axis)
    return lax.all_to_all(
        jnp.broadcast_to(shard[None], (devices, *shard.shape)), axis, 0, 0, tiled=True
    )


def taken_together(shard, axis):
    return from_everyone(shard, axis).sum(axis=0)


def together(arrays, axis):
    vector, at, gathered = (jnp.concatenate([a.reshape(-1) for a in arrays]), 0, [])
    subtotal = taken_together(vector, axis)
    for a in arrays:
        gathered.append(subtotal[at : at + a.size].reshape(a.shape))
        at += a.size
    return tuple(gathered)


def in_blocks(shard, dim, devices):
    shape = shard.shape
    blocks = shard.reshape(*shape[:dim], devices, shape[dim] // devices, *shape[dim + 1 :])
    return jnp.moveaxis(blocks, dim, 0)


def summed_on_arrival(shard, axis, dim):
    devices = lax.axis_size(axis)
    blocks = lax.all_to_all(in_blocks(shard, dim, devices), axis, 0, 0, tiled=True)
    return jnp.sum(blocks, axis=0)


def unit_stiffness():
    poisson = 0.3
    lame_first = poisson / ((1.0 + poisson) * (1.0 - 2.0 * poisson))
    shear_mod = 0.5 / (1.0 + poisson)
    elastic = np.zeros((6, 6))
    elastic[:3, :3] = lame_first
    for index in range(3):
        elastic[index, index] += 2.0 * shear_mod
        elastic[index + 3, index + 3] = shear_mod
    points = [0.5 - 0.5 / np.sqrt(3.0), 0.5 + 0.5 / np.sqrt(3.0)]
    stiffness = np.zeros((24, 24))
    for point_z in points:
        for point_y in points:
            for point_x in points:
                gradient = np.zeros((3, 8))
                for corner in range(8):
                    off_z, off_y, off_x = (corner // 4, corner // 2 % 2, corner % 2)
                    shape_x = point_x if off_x else 1.0 - point_x
                    shape_y = point_y if off_y else 1.0 - point_y
                    shape_z = point_z if off_z else 1.0 - point_z
                    sign_x = 1.0 if off_x else -1.0
                    sign_y = 1.0 if off_y else -1.0
                    sign_z = 1.0 if off_z else -1.0
                    gradient[0, corner] = sign_x * shape_y * shape_z
                    gradient[1, corner] = shape_x * sign_y * shape_z
                    gradient[2, corner] = shape_x * shape_y * sign_z
                strain_map = np.zeros((6, 24))
                for corner in range(8):
                    strain_map[0, corner] = gradient[0, corner]
                    strain_map[1, 8 + corner] = gradient[1, corner]
                    strain_map[2, 16 + corner] = gradient[2, corner]
                    strain_map[3, corner] = gradient[1, corner]
                    strain_map[3, 8 + corner] = gradient[0, corner]
                    strain_map[4, 8 + corner] = gradient[2, corner]
                    strain_map[4, 16 + corner] = gradient[1, corner]
                    strain_map[5, 16 + corner] = gradient[0, corner]
                    strain_map[5, corner] = gradient[2, corner]
                stiffness += strain_map.T @ elastic @ strain_map / 8.0
    return stiffness


def corner_offsets(corner):
    return (corner // 4, corner // 2 % 2, corner % 2)


def element_vectors(extended):
    lead = extended.ndim - 4
    padded = jnp.pad(extended, [(0, 0)] * (lead + 2) + [(0, 1), (0, 1)])
    layers = extended.shape[-3] - 1
    height = extended.shape[-2]
    width = extended.shape[-1]
    pieces = []
    for corner in range(8):
        off_z, off_y, off_x = corner_offsets(corner)
        pieces.append(
            padded[..., off_z : off_z + layers, off_y : off_y + height, off_x : off_x + width]
        )
    stacked = jnp.stack(pieces, axis=-4)
    return stacked.reshape(stacked.shape[:lead] + (24, layers, height, width))


def stiff_product(vectors, stiffness):
    return jnp.einsum("ab,...bzyx->...azyx", stiffness, vectors, precision=lax.Precision.HIGHEST)


def assemble(forces):
    lead = forces.ndim - 4
    layers, height, width = forces.shape[-3:]
    split = forces.reshape(forces.shape[:lead] + (3, 8, layers, height, width))
    total = None
    for corner in range(8):
        off_z, off_y, off_x = corner_offsets(corner)
        placed = jnp.pad(
            split[..., corner, :, :, :],
            [(0, 0)] * (lead + 1) + [(off_z, 1 - off_z), (off_y, 1 - off_y), (off_x, 1 - off_x)],
        )
        total = placed if total is None else total + placed
    return total[..., :height, :width]


def node_diagonal(padded, layers, height, width):
    total = None
    for corner in range(8):
        off_z, off_y, off_x = corner_offsets(corner)
        piece = padded[
            1 - off_z : 1 - off_z + layers,
            1 - off_y : 1 - off_y + height,
            1 - off_x : 1 - off_x + width,
        ]
        total = piece if total is None else total + piece
    return total


def inner(left, right):
    return jnp.sum(left * right, axis=(1, 2, 3, 4))


def expand(scalar):
    return scalar[:, None, None, None, None]


def shards(forward_disp, adjoint_rhs, modulus_factor, zone_base, zone_ids, fixed_mask):
    stiffness = jnp.asarray(unit_stiffness(), jnp.float32)
    labels = jnp.arange(zone_base.shape[0], dtype=jnp.int32)
    zone_scale = jnp.sum(
        jnp.where(
            zone_ids[None] == labels[:, None, None, None], zone_base[:, None, None, None], 0.0
        ),
        axis=0,
    )
    modulus = modulus_factor * zone_scale
    free = (1 - fixed_mask).astype(jnp.float32)
    layers, height, width = modulus.shape
    lower = from_behind(modulus[-1:], "space", 1)
    below_mod = jnp.concatenate([lower, modulus], axis=0)
    padded = jnp.pad(below_mod, ((0, 0), (1, 0), (1, 0)))
    diagonal = node_diagonal(padded, layers, height, width) * stiffness[0, 0]
    inverse = free / diagonal
    residual = free * adjoint_rhs
    solution = jnp.zeros_like(residual)
    precond = inverse * residual
    direction = precond
    along = precond
    step_size = None
    norm_prev = None
    for iteration in range(ITERS):
        upper = from_behind(precond[:, :, :1], "space", -1)
        extended = jnp.concatenate([precond, upper], axis=2)
        nodal = assemble(stiff_product(element_vectors(extended), stiffness) * modulus)
        spill = from_behind(nodal[:, :, layers:], "space", 1)
        own = jnp.concatenate([nodal[:, :, :1] + spill, nodal[:, :, 1:layers]], axis=2)
        image = free * own
        norm_now, curvature = together((inner(residual, precond), inner(image, precond)), "space")
        if iteration == 0:
            step_size = norm_now / curvature
            direction = precond
            along = image
        else:
            ratio = norm_now / norm_prev
            step_size = norm_now / (curvature - ratio * norm_now / step_size)
            direction = precond + expand(ratio) * direction
            along = image + expand(ratio) * along
        solution = solution + expand(step_size) * direction
        if iteration + 1 < ITERS:
            residual = residual - expand(step_size) * along
            precond = inverse * residual
        norm_prev = norm_now
    lowest = jnp.concatenate([forward_disp[:, :, :1], solution[:, :, :1]], axis=2)
    arrived = from_behind(lowest, "space", -1)
    forward_vec = element_vectors(jnp.concatenate([forward_disp, arrived[:, :, :1]], axis=2))
    solution_vec = element_vectors(jnp.concatenate([solution, arrived[:, :, 1:2]], axis=2))
    term = jnp.sum(solution_vec * stiff_product(forward_vec, stiffness), axis=(0, 1)) * zone_scale
    gradient_share = summed_on_arrival(term, "load", 1)
    return (solution, gradient_share)


def solution(mesh):
    placed = (
        P("load", None, "space", None, None),
        P("load", None, "space", None, None),
        P("space", None, None),
        P(),
        P("space", None, None),
        P("space", None, None),
    )
    return jax.shard_map(
        shards,
        mesh=mesh,
        in_specs=placed,
        out_specs=(P("load", None, "space", None, None), P("space", "load", None)),
        check_vma=False,
    )
```

profile of v0, /device:TPU:1, one launch (start us, length us, event | category | flops | bytes accessed | tf_op | source)
XLA Modules:
  0.0 141.1 jit_solution(9238782876510886379)
XLA Ops:
  0.6 1.1 select_reduce_fusion
  1.7 0.9 mul.154
  2.7 4.6 %collective-permute-start = (f32[1,128,128]{2,1,0:T(8,128)S(1)}, f32[1,128,128]{2,1,0:T(8,128)S(1)}, u32[]{:S(2)}, u32[]{:S(2)}) collective-permute-start(f32[1,128,128]{2,1,0:T(8,128)S(1)} %slice.299), channel_id=1, source_target_pairs={{0,8},{8,16},{16,24},{24,32},{32,40},{40,48},{48,56},{56,64},{64,7... | collective-permute-start | bytes 196616 | tf_op jit(solution)/shard_map/ppermute | solution.py:13
  7.3 0.9 subtract_convert_fusion
  8.2 3.4 %collective-permute-done = f32[1,128,128]{2,1,0:T(8,128)S(1)} collective-permute-done((f32[1,128,128]{2,1,0:T(8,128)S(1)}, f32[1,128,128]{2,1,0:T(8,128)S(1)}, u32[]{:S(2)}, u32[]{:S(2)}) %collective-permute-start) | collective-permute-done | bytes 65568 | tf_op jit(solution)/shard_map/ppermute | solution.py:13
  11.6 1.1 fusion.86
  12.7 1.1 bitcast_dynamic-update-slice_fusion.3
  13.8 2.1 %collective-permute-start.1 = (f32[1,3,1,128,128]{4,3,2,1,0:T(8,128)S(1)}, f32[1,3,1,128,128]{4,3,2,1,0:T(8,128)S(1)}, u32[]{:S(2)}, u32[]{:S(2)}) collective-permute-start(f32[1,3,1,128,128]{4,3,2,1,0:T(8,128)S(1)} %slice.302), channel_id=1, source_target_pairs={{8,0},{16,8},{24,16},{32,24},{40,32},{48,40},{56,48},{64,56},{72,6... | collective-permute-start | bytes 589832 | tf_op jit(solution)/shard_map/ppermute | solution.py:13
  15.9 4.9 %collective-permute-done.1 = f32[1,3,1,128,128]{4,3,2,1,0:T(8,128)S(1)} collective-permute-done((f32[1,3,1,128,128]{4,3,2,1,0:T(8,128)S(1)}, f32[1,3,1,128,128]{4,3,2,1,0:T(8,128)S(1)}, u32[]{:S(2)}, u32[]{:S(2)}) %collective-permute-start.1) | collective-permute-done | bytes 196640 | tf_op jit(solution)/shard_map/ppermute | solution.py:13
  20.8 0.2 fusion.31
  21.0 0.2 fusion.35
  21.2 0.2 fusion.37
  21.4 0.2 fusion.41
  21.7 4.6 %fusion.6 = f32[1,3,8,2,128,128]{5,2,1,4,3,0:T(8,128)S(1)} fusion(f32[24,24,1,1]{1,0,3,2:T(8,128)S(1)} %copy-done.3, f32[1,3,8,2,128,128]{5,4,3,1,2,0:T(8,128)S(1)} %fusion.41, f32[2,128,128]{2,1,0:T(8,128)S(1)} %mul.154), kind=kOutput, calls=%fused_computation.9 | convolution fusion | flops 227278848 | bytes 6424832 | tf_op jit(solution)/shard_map/ab,...bzyx->...azyx/dot_general | solution.py:110
  26.2 2.1 %fusion.91 = (f32[1,3,1,2,128,128]{5,2,1,4,3,0:T(1,128)S(1)}, f32[1,3,1,2,128,128]{5,2,1,4,3,0:T(1,128)S(1)}, f32[1,3,1,2,128,128]{5,2,1,4,3,0:T(1,128)S(1)}, f3...) fusion(f32[1,3,8,2,128,128]{5,2,1,4,3,0:T(8,128)S(1)} %fusion.6), kind=kLoop, calls=%fused_computation.172 | loop fusion | bytes 6291456 | tf_op jit(solution)/shard_map/slice | solution.py:121
  28.7 0.9 pad_add_fusion.1
  29.6 1.9 %collective-permute-start.2 = (f32[1,3,1,128,128]{4,3,2,1,0:T(8,128)S(1)}, f32[1,3,1,128,128]{4,3,2,1,0:T(8,128)S(1)}, u32[]{:S(2)}, u32[]{:S(2)}) collective-permute-start(f32[1,3,1,128,128]{4,3,2,1,0:T(8,128)S(1)} %slice.314), channel_id=1, source_target_pairs={{0,8},{8,16},{16,24},{24,32},{32,40},{40,48},{48,56},{56,64},{64,7... | collective-permute-start | bytes 589832 | tf_op jit(solution)/shard_map/ppermute | solution.py:13
  31.6 2.6 %collective-permute-done.2 = f32[1,3,1,128,128]{4,3,2,1,0:T(8,128)S(1)} collective-permute-done((f32[1,3,1,128,128]{4,3,2,1,0:T(8,128)S(1)}, f32[1,3,1,128,128]{4,3,2,1,0:T(8,128)S(1)}, u32[]{:S(2)}, u32[]{:S(2)}) %collective-permute-start.2) | collective-permute-done | bytes 196640 | tf_op jit(solution)/shard_map/ppermute | solution.py:13
  34.2 0.7 multiply_reduce_fusion.2
  35.0 1.4 pad_maximum_fusion.6
  36.4 20.6 %all_to_all.17 = f32[64,1,2]{2,1,0:T(1,128)S(1)} all-to-all(f32[64,1,2]{2,1,0:T(1,128)S(1)} %broadcast_in_dim.18), channel_id=1, replica_groups=mesh['space'=64,'load'=8] {'space'}, dimensions={0} | all-to-all | bytes 1024 | tf_op jit(solution)/shard_map/all_to_all | solution.py:18
  57.1 0.6 fusion.94
  59.1 2.8 %collective-permute-start.3 = (f32[1,3,1,128,128]{4,3,2,1,0:T(8,128)S(1)}, f32[1,3,1,128,128]{4,3,2,1,0:T(8,128)S(1)}, u32[]{:S(2)}, u32[]{:S(2)}) collective-permute-start(f32[1,3,1,128,128]{4,3,2,1,0:T(8,128)S(1)} %slice.316), channel_id=1, source_target_pairs={{8,0},{16,8},{24,16},{32,24},{40,32},{48,40},{56,48},{64,56},{72,6... | collective-permute-start | bytes 589832 | tf_op jit(solution)/shard_map/ppermute | solution.py:13
  61.8 4.2 %collective-permute-done.3 = f32[1,3,1,128,128]{4,3,2,1,0:T(8,128)S(1)} collective-permute-done((f32[1,3,1,128,128]{4,3,2,1,0:T(8,128)S(1)}, f32[1,3,1,128,128]{4,3,2,1,0:T(8,128)S(1)}, u32[]{:S(2)}, u32[]{:S(2)}) %collective-permute-start.3) | collective-permute-done | bytes 196640 | tf_op jit(solution)/shard_map/ppermute | solution.py:13
  66.3 0.2 fusion.47
  66.5 0.2 fusion.49
  66.7 0.2 fusion.53
  66.9 4.6 %fusion.3 = f32[1,3,8,2,128,128]{5,2,1,4,3,0:T(8,128)S(1)} fusion(f32[24,24,1,1]{1,0,3,2:T(8,128)S(1)} %copy-done.3, f32[1,3,8,2,128,128]{5,4,3,1,2,0:T(8,128)S(1)} %fusion.53, f32[2,128,128]{2,1,0:T(8,128)S(1)} %mul.154), kind=kOutput, calls=%fused_computation.5 | convolution fusion | flops 227278848 | bytes 6424832 | tf_op jit(solution)/shard_map/ab,...bzyx->...azyx/dot_general | solution.py:110
  71.5 2.1 %fusion.90 = (f32[1,3,1,2,128,128]{5,2,1,4,3,0:T(1,128)S(1)}, f32[1,3,1,2,128,128]{5,2,1,4,3,0:T(1,128)S(1)}, f32[1,3,1,2,128,128]{5,2,1,4,3,0:T(1,128)S(1)}, f3...) fusion(f32[1,3,8,2,128,128]{5,2,1,4,3,0:T(8,128)S(1)} %fusion.3), kind=kLoop, calls=%fused_computation.171 | loop fusion | bytes 6291456 | tf_op jit(solution)/shard_map/slice | solution.py:121
  73.9 0.9 pad_add_fusion
  74.9 2.1 %collective-permute-start.4 = (f32[1,3,1,128,128]{4,3,2,1,0:T(8,128)S(1)}, f32[1,3,1,128,128]{4,3,2,1,0:T(8,128)S(1)}, u32[]{:S(2)}, u32[]{:S(2)}) collective-permute-start(f32[1,3,1,128,128]{4,3,2,1,0:T(8,128)S(1)} %slice.328), channel_id=1, source_target_pairs={{0,8},{8,16},{16,24},{24,32},{32,40},{40,48},{48,56},{56,64},{64,7... | collective-permute-start | bytes 589832 | tf_op jit(solution)/shard_map/ppermute | solution.py:13
  76.9 2.6 %collective-permute-done.4 = f32[1,3,1,128,128]{4,3,2,1,0:T(8,128)S(1)} collective-permute-done((f32[1,3,1,128,128]{4,3,2,1,0:T(8,128)S(1)}, f32[1,3,1,128,128]{4,3,2,1,0:T(8,128)S(1)}, u32[]{:S(2)}, u32[]{:S(2)}) %collective-permute-start.4) | collective-permute-done | bytes 196640 | tf_op jit(solution)/shard_map/ppermute | solution.py:13
  79.5 0.8 multiply_reduce_fusion
  80.3 1.3 pad_maximum_fusion.7
  81.6 0.6 broadcast_in_dim.19
  82.2 8.0 %all-to-all-start.1 = ((f32[64,1,2]{2,1,0:T(1,128)}), f32[64,1,2]{2,1,0:T(1,128)S(1)}, u32[]{:S(2)}, u32[]{:S(2)}) async-start(f32[64,1,2]{2,1,0:T(1,128)} %broadcast_in_dim.19), calls=%async_computation.1 | async-start | bytes 65536 | tf_op jit(solution)/shard_map/all_to_all | solution.py:18
  90.3 9.2 %all-to-all-done.1 = f32[64,1,2]{2,1,0:T(1,128)S(1)} async-done(((f32[64,1,2]{2,1,0:T(1,128)}), f32[64,1,2]{2,1,0:T(1,128)S(1)}, u32[]{:S(2)}, u32[]{:S(2)}) %all-to-all-start.1) | async-done | bytes 544 | tf_op jit(solution)/shard_map/all_to_all | solution.py:18
  99.6 0.6 fusion.93
  105.1 2.8 %collective-permute-start.5 = (f32[1,3,2,128,128]{4,3,2,1,0:T(8,128)S(1)}, f32[1,3,2,128,128]{4,3,2,1,0:T(8,128)S(1)}, u32[]{:S(2)}, u32[]{:S(2)}) collective-permute-start(f32[1,3,2,128,128]{4,3,2,1,0:T(8,128)S(1)} %pad_maximum_fusion.4), channel_id=1, source_target_pairs={{8,0},{16,8},{24,16},{32,24},{40,32},{48,40},{56,48},{64,56},{72,6... | collective-permute-start | bytes 1179656 | tf_op jit(solution)/shard_map/ppermute | solution.py:13
  107.9 6.2 %collective-permute-done.5 = f32[1,3,2,128,128]{4,3,2,1,0:T(8,128)S(1)} collective-permute-done((f32[1,3,2,128,128]{4,3,2,1,0:T(8,128)S(1)}, f32[1,3,2,128,128]{4,3,2,1,0:T(8,128)S(1)}, u32[]{:S(2)}, u32[]{:S(2)}) %collective-permute-start.5) | collective-permute-done | bytes 393248 | tf_op jit(solution)/shard_map/ppermute | solution.py:13
  114.4 0.2 fusion.59
  114.9 0.2 fusion.65
  115.1 0.2 fusion.67
  115.3 0.2 fusion.71
  115.7 0.2 fusion.77
  115.9 6.7 %fusion = f32[2,128,128]{2,1,0:T(8,128)S(1)} fusion(f32[1,3,8,2,128,128]{5,4,3,1,2,0:T(8,128)S(1)} %fusion.65, f32[24,24,1,1]{1,0,3,2:T(8,128)S(1)} %copy-done.3, f32[1,3,8,2,128,128]{5,4,3,1,2,0:T(8,128)S(1)} %fusion.77), kind=kOutput, calls=%fused_computation.1 | convolution fusion | flops 228032512 | bytes 6424832 | tf_op jit(solution)/shard_map/ab,...bzyx->...azyx/dot_general | solution.py:110
  122.7 17.8 %all_to_all.18 = f32[8,2,16,128]{3,2,1,0:T(8,128)S(1)} all-to-all(f32[8,2,16,128]{3,2,1,0:T(8,128)S(1)} %copy.113), channel_id=1, replica_groups=mesh['space'=64,'load'=8] {'load'}, dimensions={0} | all-to-all | bytes 262144 | tf_op jit(solution)/shard_map/all_to_all | solution.py:44
  140.4 0.6 reduce_sum.101
  (61 shorter events, 2.4 us)
Async XLA Ops:
  2.7 8.9 %collective-permute-start = (f32[1,128,128]{2,1,0:T(8,128)S(1)}, f32[1,128,128]{2,1,0:T(8,128)S(1)}, u32[]{:S(2)}, u32[]{:S(2)}) collective-permute-start(f32[1,128,128]{2,1,0:T(8,128)S(1)} %slice.299), channel_id=1, source_target_pairs={{0,8},{8,16},{16,24},{24,32},{32,40},{40,48},{48,56},{56,64},{64,7... | collective-permute-start | bytes 196616 | tf_op jit(solution)/shard_map/ppermute | solution.py:13
  13.8 7.0 %collective-permute-start.1 = (f32[1,3,1,128,128]{4,3,2,1,0:T(8,128)S(1)}, f32[1,3,1,128,128]{4,3,2,1,0:T(8,128)S(1)}, u32[]{:S(2)}, u32[]{:S(2)}) collective-permute-start(f32[1,3,1,128,128]{4,3,2,1,0:T(8,128)S(1)} %slice.302), channel_id=1, source_target_pairs={{8,0},{16,8},{24,16},{32,24},{40,32},{48,40},{56,48},{64,56},{72,6... | collective-permute-start | bytes 589832 | tf_op jit(solution)/shard_map/ppermute | solution.py:13
  21.0 0.7 copy-start.3
  28.7 5.5 %copy-start = (f32[1,3,2,128,128]{4,3,2,1,0:T(8,128)S(1)}, f32[1,3,2,128,128]{4,3,2,1,0:T(8,128)}, u32[]{:S(2)}) copy-start(f32[1,3,2,128,128]{4,3,2,1,0:T(8,128)} %param.8) | copy-start | bytes 1179652
  29.6 4.5 %collective-permute-start.2 = (f32[1,3,1,128,128]{4,3,2,1,0:T(8,128)S(1)}, f32[1,3,1,128,128]{4,3,2,1,0:T(8,128)S(1)}, u32[]{:S(2)}, u32[]{:S(2)}) collective-permute-start(f32[1,3,1,128,128]{4,3,2,1,0:T(8,128)S(1)} %slice.314), channel_id=1, source_target_pairs={{0,8},{8,16},{16,24},{24,32},{32,40},{40,48},{48,56},{56,64},{64,7... | collective-permute-start | bytes 589832 | tf_op jit(solution)/shard_map/ppermute | solution.py:13
  59.1 7.0 %collective-permute-start.3 = (f32[1,3,1,128,128]{4,3,2,1,0:T(8,128)S(1)}, f32[1,3,1,128,128]{4,3,2,1,0:T(8,128)S(1)}, u32[]{:S(2)}, u32[]{:S(2)}) collective-permute-start(f32[1,3,1,128,128]{4,3,2,1,0:T(8,128)S(1)} %slice.316), channel_id=1, source_target_pairs={{8,0},{16,8},{24,16},{32,24},{40,32},{48,40},{56,48},{64,56},{72,6... | collective-permute-start | bytes 589832 | tf_op jit(solution)/shard_map/ppermute | solution.py:13
  74.8 30.2 %slice-start = ((f32[1,3,2,128,128]{4,3,2,1,0:T(8,128)}), f32[1,3,1,128,128]{4,3,2,1,0:T(8,128)S(1)}, s32[]{:S(2)}) async-start(f32[1,3,2,128,128]{4,3,2,1,0:T(8,128)} %param.7), calls=%async_computation.3 | async-start | bytes 393216 | tf_op jit(solution)/shard_map/slice | solution.py:195
  74.8 33.1 %copy-start.1 = (f32[1,3,2,128,128]{4,3,2,1,0:T(8,128)S(1)}, f32[1,3,2,128,128]{4,3,2,1,0:T(8,128)}, u32[]{:S(2)}) copy-start(f32[1,3,2,128,128]{4,3,2,1,0:T(8,128)} %param.7) | copy-start | bytes 1179652
  74.9 4.7 %collective-permute-start.4 = (f32[1,3,1,128,128]{4,3,2,1,0:T(8,128)S(1)}, f32[1,3,1,128,128]{4,3,2,1,0:T(8,128)S(1)}, u32[]{:S(2)}, u32[]{:S(2)}) collective-permute-start(f32[1,3,1,128,128]{4,3,2,1,0:T(8,128)S(1)} %slice.328), channel_id=1, source_target_pairs={{0,8},{8,16},{16,24},{24,32},{32,40},{40,48},{48,56},{56,64},{64,7... | collective-permute-start | bytes 589832 | tf_op jit(solution)/shard_map/ppermute | solution.py:13
  82.2 17.3 %all-to-all-start.1 = ((f32[64,1,2]{2,1,0:T(1,128)}), f32[64,1,2]{2,1,0:T(1,128)S(1)}, u32[]{:S(2)}, u32[]{:S(2)}) async-start(f32[64,1,2]{2,1,0:T(1,128)} %broadcast_in_dim.19), calls=%async_computation.1 | async-start | bytes 65536 | tf_op jit(solution)/shard_map/all_to_all | solution.py:18
  105.0 9.6 %copy-start.2 = (f32[1,3,2,128,128]{4,3,2,1,0:T(8,128)}, f32[1,3,2,128,128]{4,3,2,1,0:T(8,128)S(1)}, u32[]{:S(2)}) copy-start(f32[1,3,2,128,128]{4,3,2,1,0:T(8,128)S(1)} %get-tuple-element.7) | copy-start | bytes 1179652
  105.1 9.1 %collective-permute-start.5 = (f32[1,3,2,128,128]{4,3,2,1,0:T(8,128)S(1)}, f32[1,3,2,128,128]{4,3,2,1,0:T(8,128)S(1)}, u32[]{:S(2)}, u32[]{:S(2)}) collective-permute-start(f32[1,3,2,128,128]{4,3,2,1,0:T(8,128)S(1)} %pad_maximum_fusion.4), channel_id=1, source_target_pairs={{8,0},{16,8},{24,16},{32,24},{40,32},{48,40},{56,48},{64,56},{72,6... | collective-permute-start | bytes 1179656 | tf_op jit(solution)/shard_map/ppermute | solution.py:13
where the time goes:
time: 142 us; the launch traced here: 141 us
  blocking collectives  38.4 us (27%)
  waiting for transfers between devices  33.1 us (23%)
  starting transfers between devices  24.3 us (17%)
  matrix products  15.9 us (11%)
  other arithmetic  12.5 us (9%)
  local copies, waits for them, and re-layouts  9.79 us (7%)
  between operations  7.18 us (5%)
    ppermute x6, waiting for transfers between devices, from_behind(): return lax.ppermute(shard, axis, pairs)  23.9 us
    all_to_all x1, blocking collectives, from_everyone(): lax.all_to_all(jnp.broadcast_to(shard[None], (devices, *shard.shape)), ax...  20.6 us
    all_to_all x1, blocking collectives, summed_on_arrival(): lax.all_to_all(in_blocks(shard, dim, devices), axis, 0, 0, tiled=True)  17.8 us
    ppermute x6, starting transfers between devices, from_behind(): return lax.ppermute(shard, axis, pairs)  16.2 us
    dot_general x3, matrix products, stiff_product(): jnp.einsum('ab,...bzyx->...azyx', stiffness, vectors, precision=lax.Preci...  15.9 us
    all_to_all x1, waiting for transfers between devices, from_everyone(): lax.all_to_all(jnp.broadcast_to(shard[None], (devices, *shard.shape)), ax...  9.24 us
    all_to_all x1, starting transfers between devices, from_everyone(): lax.all_to_all(jnp.broadcast_to(shard[None], (devices, *shard.shape)), ax...  8.04 us
    slice x2, local copies, waits for them, and re-layouts, assemble(): split[..., corner, :, :, :]  4.29 us
  transfers between devices with their start and end apart: 7, of which 7 were waited for; matrix products, arithmetic and copies ran while one was open for 1% of the time, Pallas kernels for 0%

commit v1 on v0

v1 whole, which is shorter than its diff:
```python
import functools

import jax
import jax.numpy as jnp
import numpy as np
from jax import lax
from jax.experimental import pallas as pl
from jax.experimental.pallas import tpu as pltpu
from jax.sharding import PartitionSpec as P

F32 = jnp.float32
MESH = pl.DeviceIdType.MESH
ROWS = 128
BLOCK = 8
BLOCKS = ROWS // BLOCK

POISSON = 0.3
SHEAR = 0.5 / (1.0 + POISSON)
KAPPA = 2.0 * POISSON / (1.0 - 2.0 * POISSON)
UNIT = SHEAR / 16.0
DIAG = SHEAR * (KAPPA + 4.0) / 9.0


def shifted_down(value, lane_last):
    return jnp.where(lane_last, 0.0, pltpu.roll(value, ROWS - 1, 1))


def plane_modes(here, after, lane_last):
    total, slope = here + after, after - here
    total_next, slope_next = shifted_down(total, lane_last), shifted_down(slope, lane_last)
    return (total + total_next, total_next - total, slope + slope_next, slope_next - slope)


def strains(low, high):
    (u, v, w) = [
        (
            l[1] + h[1],
            l[2] + h[2],
            h[0] - l[0],
            l[3] + h[3],
            h[1] - l[1],
            h[2] - l[2],
            h[3] - l[3],
        )
        for l, h in zip(low, high)
    ]
    return (
        u[0], v[1], w[2],
        u[1] + v[0], u[2] + w[0], v[2] + w[1],
        u[3], w[5], u[4], v[5], v[3], w[4],
        u[5], v[4], w[3],
        u[6], v[6], w[6],
    )


def stresses(e):
    trace = KAPPA * (e[0] + e[1] + e[2])
    out = [2.0 * e[0] + trace, 2.0 * e[1] + trace, 2.0 * e[2] + trace, e[3], e[4], e[5]]
    own, cross = 1.0, KAPPA / 3.0
    for a, b in ((6, 7), (8, 9), (10, 11)):
        both = cross * (e[a] + e[b])
        out += [own * e[a] + both, own * e[b] + both]
    third = 1.0 / 3.0
    shear = (e[12] + e[13] + e[14]) * third
    out += [e[12] * third + shear, e[13] * third + shear, e[14] * third + shear]
    last = (KAPPA + 4.0) / 9.0
    out += [e[15] * last, e[16] * last, e[17] * last]
    return out


def corner_modes(f):
    return (
        (f[0], f[3], f[4], f[6], f[8], f[12], f[15]),
        (f[3], f[1], f[5], f[10], f[13], f[9], f[16]),
        (f[4], f[5], f[2], f[14], f[11], f[7], f[17]),
    )


def onto_lower(g):
    return (-g[2], g[0] - g[4], g[1] - g[5], g[3] - g[6])


def onto_upper(g):
    return (g[2], g[0] + g[4], g[1] + g[5], g[3] + g[6])


def dot(a, b):
    total = None
    for left, right in zip(a, b):
        term = left * right
        total = term if total is None else total + term
    return total


def kernel(
    fwd_hbm, rhs_hbm, fac_hbm, base_ref, ids_hbm, msk_hbm,
    x_out, grad_out,
    fac, ids, msk, rhs, fw, sc, m, y0, y1, inv, r0, r0h, ff, g0, g1, g0r, g1r,
    part, r1, mid, r2, coef, r3,
    load_sem, halo_send, halo_recv, z_send, z_recv, s1_send, s1_recv, s2_send, s2_recv, s3_send, s3_recv,
    *, spaces, loads, group,
):
    s = lax.axis_index("space")
    load = lax.axis_index("load")
    above, below = lax.rem(s + 1, spaces), lax.rem(s + spaces - 1, spaces)
    wide = spaces // group
    within, outer = lax.rem(s, group), s // group
    rows = ROWS // loads

    def local(src, dst, index):
        return pltpu.make_async_copy(src, dst, load_sem.at[index])

    loaded = [
        local(fac_hbm, fac, 0),
        local(ids_hbm, ids, 1),
        local(msk_hbm, msk, 2),
        local(rhs_hbm.at[0], rhs, 3),
        local(fwd_hbm.at[0, :, pl.ds(0, 2)], fw.at[:, pl.ds(0, 2), pl.ds(0, ROWS)], 4),
    ]
    for copy in loaded:
        copy.start()

    near = [{"space": above}, {"space": below}]
    stage1 = [lax.rem(within + i, group) for i in range(1, group)]
    stage2 = [lax.rem(outer + i, wide) for i in range(1, wide)]
    stage3 = [lax.rem(load + i, loads) for i in range(1, loads)]
    peers1 = [{"space": outer * group + i} for i in stage1]
    peers2 = [{"space": i * group + within} for i in stage2]
    peers3 = [{"load": i} for i in stage3]
    barrier = pltpu.get_barrier_semaphore()
    everyone = near + peers1 + peers2 + peers3
    for peer in everyone:
        pl.semaphore_signal(barrier, inc=1, device_id=peer, device_id_type=MESH)

    def remote(src, dst, send, recv, device):
        return pltpu.make_async_remote_copy(
            src_ref=src, dst_ref=dst, send_sem=send, recv_sem=recv, device_id=device, device_id_type=MESH
        )

    lanes = lax.broadcasted_iota(jnp.int32, (BLOCK, ROWS), 1)
    lane_first, lane_last = lanes == 0, lanes == ROWS - 1
    row_first = lax.broadcasted_iota(jnp.int32, (BLOCK, ROWS), 0) == 0
    zero = jnp.zeros((BLOCK, ROWS), F32)

    for layer in range(4):
        m[layer, 0:BLOCK, :] = zero
        for c in range(3):
            y0[layer, c, ROWS : ROWS + BLOCK, :] = zero
    for plane in range(3):
        for c in range(3):
            y1[plane, c, ROWS : ROWS + BLOCK, :] = zero
            fw[c, plane, ROWS : ROWS + BLOCK, :] = zero

    def over_blocks(body, carry=None, start=0, stop=BLOCKS):
        if carry is None:
            lax.fori_loop(start, stop, lambda b, _: (body(pl.multiple_of(b * BLOCK, BLOCK)), 0)[1], 0)
            return None
        return lax.fori_loop(start, stop, lambda b, held: body(pl.multiple_of(b * BLOCK, BLOCK), held), carry)

    loaded[0].wait()
    loaded[1].wait()
    bases = [base_ref[i] for i in range(base_ref.shape[0])]

    def moduli(row):
        for layer in range(2):
            zone = ids[layer, pl.ds(row, BLOCK), :]
            scale = jnp.full((BLOCK, ROWS), bases[0], F32)
            for i in range(1, len(bases)):
                scale = jnp.where(zone == i, bases[i], scale)
            sc[layer, pl.ds(row, BLOCK), :] = scale
            m[1 + layer, pl.ds(row + BLOCK, BLOCK), :] = fac[layer, pl.ds(row, BLOCK), :] * scale

    over_blocks(moduli)

    pl.semaphore_wait(barrier, len(everyone))
    body_rows = pl.ds(BLOCK, ROWS)
    whole = pl.ds(0, ROWS)
    m_up = remote(m.at[2, body_rows], m.at[0, body_rows], halo_send.at[0], halo_recv.at[0], {"space": above})
    m_down = remote(m.at[1, body_rows], m.at[3, body_rows], halo_send.at[1], halo_recv.at[1], {"space": below})
    m_up.start()
    m_down.start()

    loaded[2].wait()
    loaded[3].wait()

    def inverse_diagonal(low, high, row):
        here = m[low, pl.ds(row + BLOCK, BLOCK), :] + m[high, pl.ds(row + BLOCK, BLOCK), :]
        before = m[low, pl.ds(row + BLOCK - 1, BLOCK), :] + m[high, pl.ds(row + BLOCK - 1, BLOCK), :]
        total = here + before
        total = total + jnp.where(lane_first, 0.0, pltpu.roll(total, 1, 1))
        return 1.0 / (DIAG * total)

    def own_first(row):
        at = pl.ds(row, BLOCK)
        free_low = (1 - msk[0, at, :]).astype(F32)
        free_high = (1 - msk[1, at, :]).astype(F32)
        inverse = free_high * inverse_diagonal(1, 2, row)
        inv[1, at, :] = inverse
        for c in range(3):
            r0[0, c, at, :] = free_low * rhs[c, 0, at, :]
            high = free_high * rhs[c, 1, at, :]
            r0[1, c, at, :] = high
            y0[2, c, at, :] = inverse * high

    over_blocks(own_first)
    r_down = remote(r0.at[0], r0h, halo_send.at[2], halo_recv.at[2], {"space": below})
    y_up = remote(y0.at[2, :, whole], y0.at[0, :, whole], halo_send.at[3], halo_recv.at[3], {"space": above})
    r_down.start()
    y_up.start()
    loaded[4].wait()
    f_down = remote(
        fw.at[:, 0, whole], fw.at[:, 2, whole], halo_send.at[4], halo_recv.at[4], {"space": below}
    )
    f_down.start()

    def modes(ref_at, row):
        out = []
        for c in range(3):
            here, after = ref_at(c, pl.ds(row, BLOCK)), ref_at(c, pl.ds(row + 1, BLOCK))
            out.append(plane_modes(here, after, lane_last))
        return out

    def forward_stress(layer):
        def body(row):
            low = modes(lambda c, at: fw[c, layer, at, :], row)
            high = modes(lambda c, at: fw[c, layer + 1, at, :], row)
            for i, value in enumerate(stresses(strains(low, high))):
                ff[layer, i, pl.ds(row, BLOCK), :] = value

        over_blocks(body)

    forward_stress(0)

    m_up.wait_recv()
    m_down.wait_recv()
    r_down.wait_recv()
    y_up.wait_recv()

    @pl.when(s == 0)
    def _():
        m[0, BLOCK : BLOCK + ROWS, :] = jnp.zeros((ROWS, ROWS), F32)

    @pl.when(s == spaces - 1)
    def _():
        r0h[...] = jnp.zeros((3, ROWS, ROWS), F32)

    def own_second(row):
        at = pl.ds(row, BLOCK)
        inverse = (1 - msk[0, at, :]).astype(F32) * inverse_diagonal(0, 1, row)
        inv[0, at, :] = inverse
        beyond = inverse_diagonal(2, 3, row)
        for c in range(3):
            y0[1, c, at, :] = inverse * r0[0, c, at, :]
            y0[3, c, at, :] = beyond * r0h[c, at, :]

    over_blocks(own_second)

    def product(row, held):
        carried, norm, curve, next_norm = held
        at = pl.ds(row, BLOCK)
        planes = [modes(lambda c, where: y0[p, c, where, :], row) for p in range(4)]
        onto = [None, None]
        for layer in range(3):
            modulus = UNIT * m[layer, pl.ds(row + BLOCK, BLOCK), :]
            force = corner_modes([modulus * f for f in stresses(strains(planes[layer], planes[layer + 1]))])
            for plane, spread in ((layer - 1, onto_lower), (layer, onto_upper)):
                if 0 <= plane < 2:
                    new = [spread(g) for g in force]
                    if onto[plane] is None:
                        onto[plane] = new
                    else:
                        onto[plane] = [tuple(a + b for a, b in zip(o, n)) for o, n in zip(onto[plane], new)]
        passed = []
        for plane in range(2):
            inverse = inv[plane, at, :]
            for c in range(3):
                g = onto[plane][c]
                sums = (g[0] - g[1]) + jnp.where(lane_first, 0.0, pltpu.roll(g[0] + g[1], 1, 1))
                slopes = (g[2] - g[3]) + jnp.where(lane_first, 0.0, pltpu.roll(g[2] + g[3], 1, 1))
                rolled = pltpu.roll(sums + slopes, 1, 0)
                force = (sums - slopes) + jnp.where(row_first, carried[3 * plane + c], rolled)
                passed.append(rolled)
                image = inverse * force
                y1[plane, c, at, :] = image
                field = y0[1 + plane, c, at, :]
                norm = norm + r0[plane, c, at, :] * field
                curve = curve + force * field
                next_norm = next_norm + force * image
        return tuple(passed), norm, curve, next_norm

    _, norm, curve, next_norm = over_blocks(product, ((zero,) * 6, zero, zero, zero))

    y1_down = remote(y1.at[0, :, whole], y1.at[2, :, whole], halo_send.at[5], halo_recv.at[5], {"space": below})
    y1_down.start()

    def against_forward(ref, first, layer, out, energy):
        def body(row, held):
            low = modes(lambda c, at: ref[first + layer, c, at, :], row)
            high = modes(lambda c, at: ref[first + layer + 1, c, at, :], row)
            e = strains(low, high)
            at = pl.ds(row, BLOCK)
            out[layer, at, :] = UNIT * dot(e, [ff[layer, i, at, :] for i in range(18)])
            if energy:
                held = held + (UNIT * m[1 + layer, pl.ds(row + BLOCK, BLOCK), :]) * dot(e, stresses(e))
            return held

        return body

    f_down.wait_recv()

    @pl.when(s == spaces - 1)
    def _():
        fw[:, 2, 0:ROWS, :] = jnp.zeros((3, ROWS, ROWS), F32)

    forward_stress(1)
    for layer in range(2):
        over_blocks(against_forward(y0, 1, layer, g0, False), zero)

    def exchange(src, dst, sems):
        copies = []
        for slot, peer in zip(stage3, peers3):
            copy = remote(
                src.at[:, pl.ds(pl.multiple_of(slot * rows, rows), rows)], dst.at[load],
                z_send.at[sems, slot], z_recv.at[sems, load], peer,
            )
            copy.start()
            copies.append(copy)
        return copies

    sent = exchange(g0, g0r, 0)
    energy = over_blocks(against_forward(y1, 0, 0, g1, True), zero)
    y1_down.wait_recv()

    @pl.when(s == spaces - 1)
    def _():
        y1[2, :, 0:ROWS, :] = jnp.zeros((3, ROWS, ROWS), F32)

    energy = over_blocks(against_forward(y1, 0, 1, g1, True), energy)

    part[0:1, :] = jnp.sum(norm, axis=0, keepdims=True)
    part[1:2, :] = jnp.sum(curve, axis=0, keepdims=True)
    part[2:3, :] = jnp.sum(next_norm, axis=0, keepdims=True)
    part[3:4, :] = jnp.sum(energy, axis=0, keepdims=True)
    part[4:8, :] = jnp.zeros((4, ROWS), F32)
    for slot, peer in zip(stage1, peers1):
        copy = remote(part, r1.at[within], s1_send.at[slot], s1_recv.at[within], peer)
        copy.start()
        sent.append(copy)
    sent += exchange(g1, g1r, 1)
    r1[within] = part[...]

    def arrived(dst, slots, sems, like):
        for slot in slots:
            remote(like, dst.at[slot], sems.at[slot], sems.at[slot], near[0]).wait_recv()

    arrived(r1, stage1, s1_recv, part)
    total = r1[0]
    for i in range(1, group):
        total = total + r1[i]
    mid[...] = total
    for slot, peer in zip(stage2, peers2):
        copy = remote(mid, r2.at[outer], s2_send.at[slot], s2_recv.at[outer], peer)
        copy.start()
        sent.append(copy)
    r2[outer] = total
    arrived(r2, stage2, s2_recv, mid)
    total = r2[0]
    for i in range(1, wide):
        total = total + r2[i]

    sums = jnp.sum(total, axis=1, keepdims=True)
    sums = jnp.broadcast_to(sums, (BLOCK, ROWS))
    rr, rq, qq, qd = sums[0:1], sums[1:2], sums[2:3], sums[3:4]
    step = rr / rq
    norm_next = step * (step * qq) - rr
    ratio = norm_next / rr
    curve_next = rq - 2.0 * (step * qq) + step * (step * qd)
    step_next = norm_next / (curve_next - ratio * norm_next / step)
    first = step + step_next * (1.0 + ratio)
    second = -(step_next * step)
    coef[...] = jnp.concatenate([first, second, jnp.zeros((6, ROWS), F32)], axis=0)
    for slot, peer in zip(stage3, peers3):
        copy = remote(coef, r3.at[load], s3_send.at[slot], s3_recv.at[load], peer)
        copy.start()
        sent.append(copy)
    r3[load] = coef[...]
    first_all = jnp.broadcast_to(first, (BLOCK, ROWS))
    second_all = jnp.broadcast_to(second, (BLOCK, ROWS))

    def finish(row):
        at = pl.ds(row, BLOCK)
        for c in range(3):
            for plane in range(2):
                x_out[0, c, plane, at, :] = first_all * y0[1 + plane, c, at, :] + second_all * y1[plane, c, at, :]

    over_blocks(finish)

    mine = pl.ds(pl.multiple_of(load * rows, rows), rows)
    g0r[load] = g0[:, mine, :]
    g1r[load] = g1[:, mine, :]
    for slot in stage3:
        remote(g0.at[:, pl.ds(0, rows)], g0r.at[slot], z_send.at[0, slot], z_recv.at[0, slot], near[0]).wait_recv()
        remote(g1.at[:, pl.ds(0, rows)], g1r.at[slot], z_send.at[1, slot], z_recv.at[1, slot], near[0]).wait_recv()
    arrived(r3, stage3, s3_recv, coef)
    total = None
    for i in range(loads):
        term = r3[i, 0:1, :][None] * g0r[i] + r3[i, 1:2, :][None] * g1r[i]
        total = term if total is None else total + term
    grad_out[...] = sc[:, mine, :] * total

    for copy in (m_up, m_down, r_down, y_up, f_down, y1_down):
        copy.wait_send()
    for copy in sent:
        copy.wait_send()


def solution(mesh):
    spaces, loads = mesh.shape["space"], mesh.shape["load"]
    group = 16

    def shards(forward_disp, adjoint_rhs, modulus_factor, zone_base, zone_ids, fixed_mask):
        plane = (ROWS, ROWS)
        padded = (ROWS + BLOCK, ROWS)
        rows = ROWS // loads
        vmem = lambda *shape: pltpu.VMEM(shape, F32)
        ints = lambda *shape: pltpu.VMEM(shape, jnp.int32)
        dma = pltpu.SemaphoreType.DMA
        hbm = pl.BlockSpec(memory_space=pl.ANY)
        return pl.pallas_call(
            functools.partial(kernel, spaces=spaces, loads=loads, group=group),
            out_shape=(
                jax.ShapeDtypeStruct(forward_disp.shape, F32),
                jax.ShapeDtypeStruct((2, rows, ROWS), F32),
            ),
            in_specs=[hbm, hbm, hbm, pl.BlockSpec(memory_space=pltpu.SMEM), hbm, hbm],
            out_specs=(pl.BlockSpec(memory_space=pltpu.VMEM), pl.BlockSpec(memory_space=pltpu.VMEM)),
            scratch_shapes=[
                vmem(2, *plane), ints(2, *plane), ints(2, *plane), vmem(3, 2, *plane), vmem(3, 3, *padded),
                vmem(2, *plane), vmem(4, *padded), vmem(4, 3, *padded), vmem(3, 3, *padded),
                vmem(2, *plane), vmem(2, 3, *plane), vmem(3, *plane), vmem(2, 18, *plane),
                vmem(2, *plane), vmem(2, *plane), vmem(loads, 2, rows, ROWS), vmem(loads, 2, rows, ROWS),
                vmem(8, ROWS), vmem(group, 8, ROWS), vmem(8, ROWS), vmem(spaces // group, 8, ROWS),
                vmem(8, ROWS), vmem(loads, 8, ROWS),
                dma((5,)), dma((6,)), dma((6,)), dma((2, loads)), dma((2, loads)),
                dma((group,)), dma((group,)), dma((spaces // group,)), dma((spaces // group,)),
                dma((loads,)), dma((loads,)),
            ],
            compiler_params=pltpu.CompilerParams(collective_id=0, has_side_effects=True),
        )(forward_disp, adjoint_rhs, modulus_factor, zone_base, zone_ids, fixed_mask)

    placed = (
        P("load", None, "space", None, None),
        P("load", None, "space", None, None),
        P("space", None, None),
        P(),
        P("space", None, None),
        P("space", None, None),
    )
    return jax.shard_map(
        shards,
        mesh=mesh,
        in_specs=placed,
        out_specs=(P("load", None, "space", None, None), P("space", "load", None)),
        check_vma=False,
    )
```

time: 142 us -> 50.2 us (0.35)
  Pallas kernels: 0 us -> 47 us
  blocking collectives: 38.4 us -> 0 us
  waiting for transfers between devices: 33.1 us -> 0 us
  starting transfers between devices: 24.3 us -> 0 us
  matrix products: 15.9 us -> 0 us
  other arithmetic: 12.5 us -> 0 us
  local copies, waits for them, and re-layouts: 9.79 us -> 2.38 us
  between operations: 7.18 us -> 0.65 us
    pallas_call x0 -> x1, Pallas kernels: none -> 47 us  [shards(): pl.pallas_call(functools.partial(kernel, spaces=spaces, loads=loads, grou...]
    all_to_all x2 -> x0, blocking collectives: 38.4 us -> none  [the longest x1 20.6 us: from_everyone(): lax.all_to_all(jnp.broadcast_to(shard[None], (devices, *shard.shape)), ax...]
    ppermute x6 -> x0, waiting for transfers between devices: 23.9 us -> none  [from_behind(): return lax.ppermute(shard, axis, pairs)]
    ppermute x6 -> x0, starting transfers between devices: 16.2 us -> none  [from_behind(): return lax.ppermute(shard, axis, pairs)]
    dot_general x3 -> x0, matrix products: 15.9 us -> none  [stiff_product(): jnp.einsum('ab,...bzyx->...azyx', stiffness, vectors, precision=lax.Preci...]
    all_to_all x1 -> x0, waiting for transfers between devices: 9.24 us -> none  [from_everyone(): lax.all_to_all(jnp.broadcast_to(shard[None], (devices, *shard.shape)), ax...]
    all_to_all x1 -> x0, starting transfers between devices: 8.04 us -> none  [from_everyone(): lax.all_to_all(jnp.broadcast_to(shard[None], (devices, *shard.shape)), ax...]
    slice x13 -> x0, local copies, waits for them, and re-layouts: 5.58 us -> none  [the longest x2 4.29 us: assemble(): split[..., corner, :, :, :]]
  transfers between devices with their start and end apart: 7 -> 0, of which waited for: 7 -> 0; matrix products, arithmetic and copies ran while one was open for 1% -> 0% of each run, Pallas kernels for 0% -> 0%
where the time goes in v1:
time: 50.2 us; the launch traced here: 50 us
  Pallas kernels  47 us (94%)
  local copies, waits for them, and re-layouts  2.38 us (5%)
  between operations  0.65 us (1%)
    pallas_call x1, Pallas kernels, shards(): pl.pallas_call(functools.partial(kernel, spaces=spaces, loads=loads, grou...  47 us
    unnamed x4, local copies, waits for them, and re-layouts  2.38 us

profile of v1, /device:TPU:1, one launch (start us, length us, event | category | flops | bytes accessed | tf_op | source)
XLA Modules:
  0.0 50.0 jit_solution(4664609491045987184)
XLA Ops:
  0.6 47.0 %shard_map.77 = (f32[1,3,2,128,128]{4,3,2,1,0:T(8,128)}, f32[2,16,128]{2,1,0:T(8,128)}) custom-call(f32[1,3,2,128,128]{4,3,2,1,0:T(8,128)} %fwd_hbm.1, f32[1,3,2,128,128]{4,3,2,1,0:T(8,128)} %rhs_hbm.1, f32[2,128,128]{2,1,0:T(8,128)} %fac_hbm.1, f32[8]{0:T(128)} %base_ref.1, s32[2,128,128]{2,1,0:T(8,128)} %ids_hbm.1, s32[2,128,128]{2,1,0:T(8,128)} %msk_hbm.1), custom_call_target="tpu_custom_call" | custom-call | tf_op jit(solution)/shard_map/pallas_call | solution.py:429
  47.6 0.0 copy-start
  47.6 1.8 %copy.10 = f32[1,3,2,128,128]{4,3,2,1,0:T(8,128)} copy(f32[1,3,2,128,128]{4,3,2,1,0:T(8,128)} %get-tuple-element.4) | data formatting | bytes 786432
  49.4 0.0 copy-done
  49.4 0.6 %copy.11 = f32[2,16,128]{2,1,0:T(8,128)} copy(f32[2,16,128]{2,1,0:T(8,128)S(1)} %copy-done) | data formatting | bytes 32768
Async XLA Ops:
  47.6 1.8 %copy-start = (f32[2,16,128]{2,1,0:T(8,128)S(1)}, f32[2,16,128]{2,1,0:T(8,128)}, u32[]{:S(2)}) copy-start(f32[2,16,128]{2,1,0:T(8,128)} %get-tuple-element.5) | copy-start | bytes 49156

commit v2 on v1

v2 whole, which is shorter than its diff:
```python
import functools

import jax
import jax.numpy as jnp
import numpy as np
from jax import lax
from jax.experimental import pallas as pl
from jax.experimental.pallas import tpu as pltpu
from jax.sharding import PartitionSpec as P

F32 = jnp.float32
MESH = pl.DeviceIdType.MESH
ROWS = 128
TILE = 8
LIMIT = 40 * 2**20

POISSON = 0.3
SHEAR = 0.5 / (1.0 + POISSON)
KAPPA = 2.0 * POISSON / (1.0 - 2.0 * POISSON)
UNIT = SHEAR / 16.0
DIAG = SHEAR * (KAPPA + 4.0) / 9.0


def shifted_down(value):
    last = lax.broadcasted_iota(jnp.int32, value.shape, 1) == ROWS - 1
    return jnp.where(last, 0.0, pltpu.roll(value, ROWS - 1, 1))


def shifted_up(value):
    first = lax.broadcasted_iota(jnp.int32, value.shape, 1) == 0
    return jnp.where(first, 0.0, pltpu.roll(value, 1, 1))


def plane_modes(here, after):
    total, slope = here + after, after - here
    total_next, slope_next = shifted_down(total), shifted_down(slope)
    return (total + total_next, total_next - total, slope + slope_next, slope_next - slope)


def strains(low, high):
    (u, v, w) = [
        (
            l[1] + h[1],
            l[2] + h[2],
            h[0] - l[0],
            l[3] + h[3],
            h[1] - l[1],
            h[2] - l[2],
            h[3] - l[3],
        )
        for l, h in zip(low, high)
    ]
    return (
        u[0], v[1], w[2],
        u[1] + v[0], u[2] + w[0], v[2] + w[1],
        u[3], w[5], u[4], v[5], v[3], w[4],
        u[5], v[4], w[3],
        u[6], v[6], w[6],
    )


def stresses(e):
    trace = KAPPA * (e[0] + e[1] + e[2])
    out = [2.0 * e[0] + trace, 2.0 * e[1] + trace, 2.0 * e[2] + trace, e[3], e[4], e[5]]
    own, cross = 1.0, KAPPA / 3.0
    for a, b in ((6, 7), (8, 9), (10, 11)):
        both = cross * (e[a] + e[b])
        out += [own * e[a] + both, own * e[b] + both]
    third = 1.0 / 3.0
    shear = (e[12] + e[13] + e[14]) * third
    out += [e[12] * third + shear, e[13] * third + shear, e[14] * third + shear]
    last = (KAPPA + 4.0) / 9.0
    out += [e[15] * last, e[16] * last, e[17] * last]
    return out


def corner_modes(f):
    return (
        (f[0], f[3], f[4], f[6], f[8], f[12], f[15]),
        (f[3], f[1], f[5], f[10], f[13], f[9], f[16]),
        (f[4], f[5], f[2], f[14], f[11], f[7], f[17]),
    )


def onto_lower(g):
    return (-g[2], g[0] - g[4], g[1] - g[5], g[3] - g[6])


def onto_upper(g):
    return (g[2], g[0] + g[4], g[1] + g[5], g[3] + g[6])


def dot(a, b):
    total = None
    for left, right in zip(a, b):
        term = left * right
        total = term if total is None else total + term
    return total


def folded(value):
    total = value[0:TILE]
    for i in range(1, value.shape[0] // TILE):
        total = total + value[i * TILE : (i + 1) * TILE]
    return total


def over_rows(body, size, carry=None):
    at = lambda b: pl.multiple_of(b * size, size)
    if carry is None:
        lax.fori_loop(0, ROWS // size, lambda b, _: (body(at(b)), 0)[1], 0)
        return None
    return lax.fori_loop(0, ROWS // size, lambda b, held: body(at(b), held), carry)


def kernel(
    fwd_hbm, rhs_hbm, fac_hbm, base_hbm, ids_hbm, msk_hbm,
    y0, y1, coef, gsum, scale_out,
    base, fac, ids, msk, rhs, fw, sc, m, y0h, y1h, inv, r0, r0h, ff, g0, g1, g0r, g1r,
    part, r1, mid, r2, r3,
    load_sem, halo_send, halo_recv, z_send, z_recv, s1_send, s1_recv, s2_send, s2_recv, s3_send, s3_recv,
    *, spaces, loads, group,
):
    s = lax.axis_index("space")
    load = lax.axis_index("load")
    above, below = lax.rem(s + 1, spaces), lax.rem(s + spaces - 1, spaces)
    wide = spaces // group
    within, outer = lax.rem(s, group), s // group
    rows = ROWS // loads

    def local(src, dst, index):
        return pltpu.make_async_copy(src, dst, load_sem.at[index])

    loaded = [
        local(base_hbm, base, 5),
        local(fac_hbm, fac, 0),
        local(ids_hbm, ids, 1),
        local(msk_hbm, msk, 2),
        local(rhs_hbm.at[0], rhs, 3),
        local(fwd_hbm.at[0, :, pl.ds(0, 2)], fw.at[:, pl.ds(0, 2), pl.ds(0, ROWS)], 4),
    ]
    for copy in loaded:
        copy.start()

    near = [{"space": above}, {"space": below}]
    stage1 = [lax.rem(within + i, group) for i in range(1, group)]
    stage2 = [lax.rem(outer + i, wide) for i in range(1, wide)]
    stage3 = [lax.rem(load + i, loads) for i in range(1, loads)]
    peers1 = [{"space": outer * group + i} for i in stage1]
    peers2 = [{"space": i * group + within} for i in stage2]
    peers3 = [{"load": i} for i in stage3]
    barrier = pltpu.get_barrier_semaphore()
    everyone = near + peers1 + peers2 + peers3
    for peer in everyone:
        pl.semaphore_signal(barrier, inc=1, device_id=peer, device_id_type=MESH)

    def remote(src, dst, send, recv, device):
        return pltpu.make_async_remote_copy(
            src_ref=src, dst_ref=dst, send_sem=send, recv_sem=recv, device_id=device, device_id_type=MESH
        )

    zero = jnp.zeros((TILE, ROWS), F32)
    past = slice(ROWS, ROWS + TILE)
    for layer in range(4):
        m[layer, 0:TILE, :] = zero
    for c in range(3):
        y1h[c, past, :] = zero
        for plane in range(2):
            y0[c, plane, past, :] = zero
            y0h[c, plane, past, :] = zero
            y1[c, plane, past, :] = zero
        for plane in range(3):
            fw[c, plane, past, :] = zero

    for copy in loaded[:3]:
        copy.wait()
    bases = [base[i] for i in range(base.shape[0])]

    def moduli(row, n=16):
        at = pl.ds(row, n)
        for layer in range(2):
            zone = ids[layer, at, :]
            scale = jnp.full((n, ROWS), bases[0], F32)
            for i in range(1, len(bases)):
                scale = jnp.where(zone == i, bases[i], scale)
            sc[layer, at, :] = scale
            m[1 + layer, pl.ds(row + TILE, n), :] = fac[layer, at, :] * scale

    over_rows(moduli, 16)
    loaded[3].wait()
    loaded[4].wait()

    def inverse_diagonal(low, high, row, n):
        here = m[low, pl.ds(row + TILE, n), :] + m[high, pl.ds(row + TILE, n), :]
        before = m[low, pl.ds(row + TILE - 1, n), :] + m[high, pl.ds(row + TILE - 1, n), :]
        total = here + before
        return 1.0 / (DIAG * (total + shifted_up(total)))

    def own_first(row, n=64):
        at = pl.ds(row, n)
        free_low = (1 - msk[0, at, :]).astype(F32)
        free_high = (1 - msk[1, at, :]).astype(F32)
        inverse = free_high * inverse_diagonal(1, 2, row, n)
        inv[1, at, :] = inverse
        for c in range(3):
            r0[c, 0, at, :] = free_low * rhs[c, 0, at, :]
            high = free_high * rhs[c, 1, at, :]
            r0[c, 1, at, :] = high
            y0[c, 1, at, :] = inverse * high

    over_rows(own_first, 64)

    pl.semaphore_wait(barrier, len(everyone))
    body_rows = pl.ds(TILE, ROWS)
    whole = pl.ds(0, ROWS)
    m_up = remote(m.at[2, body_rows], m.at[0, body_rows], halo_send.at[0], halo_recv.at[0], {"space": above})
    m_down = remote(m.at[1, body_rows], m.at[3, body_rows], halo_send.at[1], halo_recv.at[1], {"space": below})
    m_up.start()
    m_down.start()
    r_down = remote(r0.at[:, 0], r0h, halo_send.at[2], halo_recv.at[2], {"space": below})
    y_up = remote(y0.at[:, 1, whole], y0h.at[:, 0, whole], halo_send.at[3], halo_recv.at[3], {"space": above})
    r_down.start()
    y_up.start()
    loaded[5].wait()
    f_down = remote(
        fw.at[:, 0, whole], fw.at[:, 2, whole], halo_send.at[4], halo_recv.at[4], {"space": below}
    )
    f_down.start()

    def modes(plane, row, n):
        return [plane_modes(ref[pl.ds(row, n), :], ref[pl.ds(row + 1, n), :]) for ref in plane]

    y0_planes = [
        [y0h.at[c, 0] for c in range(3)],
        [y0.at[c, 0] for c in range(3)],
        [y0.at[c, 1] for c in range(3)],
        [y0h.at[c, 1] for c in range(3)],
    ]
    y1_planes = [
        [y1.at[c, 0] for c in range(3)],
        [y1.at[c, 1] for c in range(3)],
        [y1h.at[c] for c in range(3)],
    ]

    def forward_stress(layer, n):
        def body(row):
            low = modes([fw.at[c, layer] for c in range(3)], row, n)
            high = modes([fw.at[c, layer + 1] for c in range(3)], row, n)
            for i, value in enumerate(stresses(strains(low, high))):
                ff[layer, i, pl.ds(row, n), :] = value

        over_rows(body, n)

    forward_stress(0, 32)

    m_up.wait_recv()
    m_down.wait_recv()
    r_down.wait_recv()
    y_up.wait_recv()

    @pl.when(s == 0)
    def _():
        m[0, TILE : TILE + ROWS, :] = jnp.zeros((ROWS, ROWS), F32)

    @pl.when(s == spaces - 1)
    def _():
        r0h[...] = jnp.zeros((3, ROWS, ROWS), F32)

    def own_second(row, n=64):
        at = pl.ds(row, n)
        inverse = (1 - msk[0, at, :]).astype(F32) * inverse_diagonal(0, 1, row, n)
        inv[0, at, :] = inverse
        beyond = inverse_diagonal(2, 3, row, n)
        for c in range(3):
            y0[c, 0, at, :] = inverse * r0[c, 0, at, :]
            y0h[c, 1, at, :] = beyond * r0h[c, at, :]

    over_rows(own_second, 64)

    def product(row, held, n=16):
        carried, norm, curve, next_norm = held
        at = pl.ds(row, n)
        row_first = lax.broadcasted_iota(jnp.int32, (TILE, ROWS), 0) == 0
        planes = [modes(plane, row, n) for plane in y0_planes]
        onto = [None, None]
        for layer in range(3):
            modulus = UNIT * m[layer, pl.ds(row + TILE, n), :]
            force = corner_modes([modulus * f for f in stresses(strains(planes[layer], planes[layer + 1]))])
            for plane, spread in ((layer - 1, onto_lower), (layer, onto_upper)):
                if 0 <= plane < 2:
                    new = [spread(g) for g in force]
                    if onto[plane] is None:
                        onto[plane] = new
                    else:
                        onto[plane] = [tuple(a + b for a, b in zip(o, w)) for o, w in zip(onto[plane], new)]
        passed = []
        for plane in range(2):
            inverse = inv[plane, at, :]
            for c in range(3):
                g = onto[plane][c]
                sums = (g[0] - g[1]) + shifted_up(g[0] + g[1])
                slopes = (g[2] - g[3]) + shifted_up(g[2] + g[3])
                rolled = pltpu.roll(sums + slopes, 1, 0)
                head = jnp.where(row_first, carried[3 * plane + c], rolled[0:TILE])
                passed.append(rolled[0:TILE])
                if n > TILE:
                    head = jnp.concatenate([head, rolled[TILE:n]], axis=0)
                force = (sums - slopes) + head
                image = inverse * force
                y1[c, plane, at, :] = image
                field = y0[c, plane, at, :]
                norm = norm + folded(r0[c, plane, at, :] * field)
                curve = curve + folded(force * field)
                next_norm = next_norm + folded(force * image)
        return tuple(passed), norm, curve, next_norm

    _, norm, curve, next_norm = over_rows(product, 16, ((zero,) * 6, zero, zero, zero))

    y1_down = remote(y1.at[:, 0, whole], y1h.at[:, whole], halo_send.at[5], halo_recv.at[5], {"space": below})
    y1_down.start()

    def against_forward(planes, first, out, energy, n):
        def body(row, held):
            all_modes = [modes(plane, row, n) for plane in planes]
            at = pl.ds(row, n)
            for i in range(len(planes) - 1):
                layer = first + i
                e = strains(all_modes[i], all_modes[i + 1])
                out[layer, at, :] = UNIT * dot(e, [ff[layer, j, at, :] for j in range(18)])
                if energy:
                    held = held + folded((UNIT * m[1 + layer, pl.ds(row + TILE, n), :]) * dot(e, stresses(e)))
            return held

        return lambda held: over_rows(body, n, held)

    f_down.wait_recv()

    @pl.when(s == spaces - 1)
    def _():
        fw[:, 2, 0:ROWS, :] = jnp.zeros((3, ROWS, ROWS), F32)

    forward_stress(1, 32)
    against_forward(y0_planes[1:4], 0, g0, False, 16)(zero)

    def exchange(src, dst, sems):
        copies = []
        for slot, peer in zip(stage3, peers3):
            copy = remote(
                src.at[:, pl.ds(pl.multiple_of(slot * rows, rows), rows)], dst.at[load],
                z_send.at[sems, slot], z_recv.at[sems, load], peer,
            )
            copy.start()
            copies.append(copy)
        return copies

    sent = exchange(g0, g0r, 0)
    energy = against_forward(y1_planes[0:2], 0, g1, True, 32)(zero)
    y1_down.wait_recv()

    @pl.when(s == spaces - 1)
    def _():
        y1h[:, 0:ROWS, :] = jnp.zeros((3, ROWS, ROWS), F32)

    energy = against_forward(y1_planes[1:3], 1, g1, True, 32)(energy)

    part[0:1, :] = jnp.sum(norm, axis=0, keepdims=True)
    part[1:2, :] = jnp.sum(curve, axis=0, keepdims=True)
    part[2:3, :] = jnp.sum(next_norm, axis=0, keepdims=True)
    part[3:4, :] = jnp.sum(energy, axis=0, keepdims=True)
    part[4:8, :] = jnp.zeros((4, ROWS), F32)
    for slot, peer in zip(stage1, peers1):
        copy = remote(part, r1.at[within], s1_send.at[slot], s1_recv.at[within], peer)
        copy.start()
        sent.append(copy)
    sent += exchange(g1, g1r, 1)
    r1[within] = part[...]

    def arrived(dst, slots, sems, like):
        for slot in slots:
            remote(like, dst.at[slot], sems.at[slot], sems.at[slot], near[0]).wait_recv()

    arrived(r1, stage1, s1_recv, part)
    total = r1[0]
    for i in range(1, group):
        total = total + r1[i]
    mid[...] = total
    for slot, peer in zip(stage2, peers2):
        copy = remote(mid, r2.at[outer], s2_send.at[slot], s2_recv.at[outer], peer)
        copy.start()
        sent.append(copy)
    r2[outer] = total
    arrived(r2, stage2, s2_recv, mid)
    total = r2[0]
    for i in range(1, wide):
        total = total + r2[i]

    sums = jnp.sum(total, axis=1, keepdims=True)
    sums = jnp.broadcast_to(sums, (TILE, ROWS))
    rr, rq, qq, qd = sums[0:1], sums[1:2], sums[2:3], sums[3:4]
    step = rr / rq
    norm_next = step * (step * qq) - rr
    ratio = norm_next / rr
    curve_next = rq - 2.0 * (step * qq) + step * (step * qd)
    step_next = norm_next / (curve_next - ratio * norm_next / step)
    first = step + step_next * (1.0 + ratio)
    second = -(step_next * step)
    coef[...] = jnp.concatenate([first, second, jnp.zeros((6, ROWS), F32)], axis=0)
    for slot, peer in zip(stage3, peers3):
        copy = remote(coef, r3.at[load], s3_send.at[slot], s3_recv.at[load], peer)
        copy.start()
        sent.append(copy)
    r3[load] = coef[...]

    mine = pl.ds(pl.multiple_of(load * rows, rows), rows)
    g0r[load] = g0[:, mine, :]
    g1r[load] = g1[:, mine, :]
    scale_out[...] = sc[:, mine, :]
    for slot in stage3:
        remote(g0.at[:, pl.ds(0, rows)], g0r.at[slot], z_send.at[0, slot], z_recv.at[0, slot], near[0]).wait_recv()
        remote(g1.at[:, pl.ds(0, rows)], g1r.at[slot], z_send.at[1, slot], z_recv.at[1, slot], near[0]).wait_recv()
    arrived(r3, stage3, s3_recv, coef)
    total = None
    for i in range(loads):
        term = r3[i, 0:1, :][None] * g0r[i] + r3[i, 1:2, :][None] * g1r[i]
        total = term if total is None else total + term
    gsum[...] = total

    for copy in (m_up, m_down, r_down, y_up, f_down, y1_down):
        copy.wait_send()
    for copy in sent:
        copy.wait_send()


def finish(y0, y1, coef, gsum, scale, x_out, grad_out, x, grad, sem):
    grad[...] = scale[...] * gsum[...]
    copies = [pltpu.make_async_copy(grad, grad_out, sem.at[3])]
    copies[0].start()
    first = jnp.broadcast_to(coef[0:1, :], (ROWS, ROWS))
    second = jnp.broadcast_to(coef[1:2, :], (ROWS, ROWS))
    for c in range(3):
        for plane in range(2):
            x[c, plane] = first * y0[c, plane, 0:ROWS, :] + second * y1[c, plane, 0:ROWS, :]
        copy = pltpu.make_async_copy(x.at[c], x_out.at[0, c], sem.at[c])
        copy.start()
        copies.append(copy)
    for copy in copies:
        copy.wait()


def solution(mesh):
    spaces, loads = mesh.shape["space"], mesh.shape["load"]
    group = 16
    rows = ROWS // loads

    def shards(forward_disp, adjoint_rhs, modulus_factor, zone_base, zone_ids, fixed_mask):
        plane = (ROWS, ROWS)
        padded = (ROWS + TILE, ROWS)
        vmem = lambda *shape: pltpu.VMEM(shape, F32)
        ints = lambda *shape: pltpu.VMEM(shape, jnp.int32)
        dma = pltpu.SemaphoreType.DMA
        hbm = pl.BlockSpec(memory_space=pltpu.HBM)
        held = pl.BlockSpec(memory_space=pltpu.VMEM)
        out = lambda *shape: jax.ShapeDtypeStruct(shape, F32)
        pinned = [
            pltpu.with_memory_space_constraint(a, pltpu.HBM)
            for a in (forward_disp, adjoint_rhs, modulus_factor, zone_base, zone_ids, fixed_mask)
        ]
        y0, y1, coef, gsum, scale = pl.pallas_call(
            functools.partial(kernel, spaces=spaces, loads=loads, group=group),
            out_shape=(
                out(3, 2, *padded), out(3, 2, *padded), out(TILE, ROWS), out(2, rows, ROWS), out(2, rows, ROWS)
            ),
            in_specs=[hbm] * 6,
            out_specs=(held,) * 5,
            scratch_shapes=[
                pltpu.SMEM(zone_base.shape, F32),
                vmem(2, *plane), ints(2, *plane), ints(2, *plane), vmem(3, 2, *plane), vmem(3, 3, *padded),
                vmem(2, *plane), vmem(4, *padded), vmem(3, 2, *padded), vmem(3, *padded),
                vmem(2, *plane), vmem(3, 2, *plane), vmem(3, *plane), vmem(2, 18, *plane),
                vmem(2, *plane), vmem(2, *plane), vmem(loads, 2, rows, ROWS), vmem(loads, 2, rows, ROWS),
                vmem(TILE, ROWS), vmem(group, TILE, ROWS), vmem(TILE, ROWS), vmem(spaces // group, TILE, ROWS),
                vmem(loads, TILE, ROWS),
                dma((6,)), dma((6,)), dma((6,)), dma((2, loads)), dma((2, loads)),
                dma((group,)), dma((group,)), dma((spaces // group,)), dma((spaces // group,)),
                dma((loads,)), dma((loads,)),
            ],
            compiler_params=pltpu.CompilerParams(collective_id=0, has_side_effects=True, vmem_limit_bytes=LIMIT),
        )(*pinned)
        return pl.pallas_call(
            finish,
            out_shape=(out(1, 3, 2, *plane), out(2, rows, ROWS)),
            in_specs=[held] * 5,
            out_specs=(hbm, hbm),
            scratch_shapes=[vmem(3, 2, *plane), vmem(2, rows, ROWS), dma((4,))],
            compiler_params=pltpu.CompilerParams(vmem_limit_bytes=4 * 2**20),
        )(y0, y1, coef, gsum, scale)

    placed = (
        P("load", None, "space", None, None),
        P("load", None, "space", None, None),
        P("space", None, None),
        P(),
        P("space", None, None),
        P("space", None, None),
    )
    return jax.shard_map(
        shards,
        mesh=mesh,
        in_specs=placed,
        out_specs=(P("load", None, "space", None, None), P("space", "load", None)),
        check_vma=False,
    )
```

time: 50.2 us -> 42.4 us (0.84)
  Pallas kernels: 47 us -> 41.1 us
  local copies, waits for them, and re-layouts: 2.38 us -> 0 us
    pallas_call x1, Pallas kernels: 47 us -> 40.3 us  [shards(): pl.pallas_call(functools.partial(kernel, spaces=spaces, loads=loads, grou...]
    unnamed x4 -> x0, local copies, waits for them, and re-layouts: 2.38 us -> none
    pallas_call x0 -> x1, Pallas kernels: none -> 0.81 us  [shards(): pl.pallas_call(finish, out_shape=(out(1, 3, 2, *plane), out(2, rows, ROWS...]
where the time goes in v2:
time: 42.4 us; the launch traced here: 41.7 us
  Pallas kernels  41.1 us (97%)
  between operations  0.64 us (2%)
    pallas_call x1, Pallas kernels, shards(): pl.pallas_call(functools.partial(kernel, spaces=spaces, loads=loads, grou...  40.3 us

profile of v2, /device:TPU:1, one launch (start us, length us, event | category | flops | bytes accessed | tf_op | source)
XLA Modules:
  0.0 41.7 jit_solution(9103230198294133816)
XLA Ops:
  0.6 40.3 %shard_map.77 = (f32[3,2,136,128]{3,2,1,0:T(8,128)S(1)}, f32[3,2,136,128]{3,2,1,0:T(8,128)S(1)}, f32[8,128]{1,0:T(8,128)S(1)}, f32[2,16,128]{2,1,0:T(8,128)S(1)}, f32[2,16,128]{2,1,0:T(8,128)S(1)}) custom-call(f32[1,3,2,128,128]{4,3,2,1,0:T(8,128)} %fwd_hbm.1, f32[1,3,2,128,128]{4,3,2,1,0:T(8,128)} %rhs_hbm.1, f32[2,128,128]{2,1,0:T(8,128)} %fac_hbm.1, ...), custom_call_target="tpu_custom_call" | custom-call | tf_op jit(solution)/shard_map/pallas_call | solution.py:468
  40.9 0.8 %shard_map.78 = (f32[1,3,2,128,128]{4,3,2,1,0:T(8,128)}, f32[2,16,128]{2,1,0:T(8,128)}) custom-call(f32[3,2,136,128]{3,2,1,0:T(8,128)S(1)} %get-tuple-element.7.y0, f32[3,2,136,128]{3,2,1,0:T(8,128)S(1)} %get-tuple-element.8.y1, f32[8,128]{1,0:T(8,128)S(1)} %get-tuple-element.9.coef, f32[2,16,128]{2,1,0:T(8,128)S(1)} %get-tuple-element.10.gsum, ...), custom_call_target="tpu_custom_call" | custom-call | tf_op jit(solution)/shard_map/pallas_call | solution.py:489

commit v3 on v2

--- a/solution.py
+++ b/solution.py
@@ -12,6 +12,11 @@
 MESH = pl.DeviceIdType.MESH
 ROWS = 128
 TILE = 8
+LONG = 8
+STEP = 16
+CHUNKS = 4
+CHUNK = ROWS // CHUNKS
+DONE = [0] + [(i + 1) * CHUNK - STEP for i in range(CHUNKS - 1)] + [ROWS]
 LIMIT = 40 * 2**20
 
 POISSON = 0.3
@@ -105,20 +110,21 @@
     return total
 
 
-def over_rows(body, size, carry=None):
+def over_rows(body, size, carry=None, start=0, stop=ROWS):
     at = lambda b: pl.multiple_of(b * size, size)
+    first, last = start // size, stop // size
     if carry is None:
-        lax.fori_loop(0, ROWS // size, lambda b, _: (body(at(b)), 0)[1], 0)
+        lax.fori_loop(first, last, lambda b, _: (body(at(b)), 0)[1], 0)
         return None
-    return lax.fori_loop(0, ROWS // size, lambda b, held: body(at(b), held), carry)
+    return lax.fori_loop(first, last, lambda b, held: body(at(b), held), carry)
 
 
 def kernel(
     fwd_hbm, rhs_hbm, fac_hbm, base_hbm, ids_hbm, msk_hbm,
-    y0, y1, coef, gsum, scale_out,
-    base, fac, ids, msk, rhs, fw, sc, m, y0h, y1h, inv, r0, r0h, ff, g0, g1, g0r, g1r,
-    part, r1, mid, r2, r3,
-    load_sem, halo_send, halo_recv, z_send, z_recv, s1_send, s1_recv, s2_send, s2_recv, s3_send, s3_recv,
+    x_out, grad_out,
+    base, fac, ids, msk, rhs, fw, sc, m, y0, y1, y0h, y1h, inv, r0, r0h, ff, g0, g1, g0r, g1r,
+    part, r1, mid, r2, coefs,
+    load_sem, halo_send, halo_recv, z_send, z_recv, s1_send, s1_recv, s2_send, s2_recv, known1, known2, known3,
     *, spaces, loads, group,
 ):
     s = lax.axis_index("space")
@@ -142,17 +148,30 @@
     for copy in loaded:
         copy.start()
 
-    near = [{"space": above}, {"space": below}]
+    core, y = lax.rem(s, 2), lax.rem(s // 2, LONG)
+    at_y = lambda step, c: {"space": outer * group + lax.rem(y + LONG + step, LONG) * 2 + c}
+    at_x = lambda step: {"space": lax.rem(outer + wide + step, wide) * group + within}
+    at_z = lambda step: {"load": lax.rem(load + loads + step, loads)}
+
+    near = [{"space": above}, {"space": below}, at_y(0, 1 - core)]
+    near += [at_y(step, c) for step in (1, -1) for c in range(2)] + [at_x(1), at_x(-1), at_z(1), at_z(-1)]
+    next1 = [at_y(1, core), at_y(-1, core), at_x(1), at_x(-1), at_z(1), at_z(-1)]
+    next2 = [at_y(2, core), at_y(-2, core), at_z(2), at_z(-2)]
+    next3 = [at_x(1), at_x(-1), at_x(2)]
+
+    def tell(sem, peers):
+        for peer in peers:
+            pl.semaphore_signal(sem, inc=1, device_id=peer, device_id_type=MESH)
+
+    barrier = pltpu.get_barrier_semaphore()
+    tell(barrier, near)
+
     stage1 = [lax.rem(within + i, group) for i in range(1, group)]
-    stage2 = [lax.rem(outer + i, wide) for i in range(1, wide)]
+    peers1 = [{"space": outer * group + i} for i in stage1]
+    stage2 = [(lax.rem(outer + i, wide), lax.rem(load + j, loads)) for i in range(wide) for j in range(loads)][1:]
+    peers2 = [{"space": i * group + within, "load": j} for i, j in stage2]
     stage3 = [lax.rem(load + i, loads) for i in range(1, loads)]
-    peers1 = [{"space": outer * group + i} for i in stage1]
-    peers2 = [{"space": i * group + within} for i in stage2]
     peers3 = [{"load": i} for i in stage3]
-    barrier = pltpu.get_barrier_semaphore()
-    everyone = near + peers1 + peers2 + peers3
-    for peer in everyone:
-        pl.semaphore_signal(barrier, inc=1, device_id=peer, device_id_type=MESH)
 
     def remote(src, dst, send, recv, device):
         return pltpu.make_async_remote_copy(
@@ -210,22 +229,83 @@
 
     over_rows(own_first, 64)
 
-    pl.semaphore_wait(barrier, len(everyone))
+    pl.semaphore_wait(barrier, len(near))
+    tell(known1, next1)
     body_rows = pl.ds(TILE, ROWS)
     whole = pl.ds(0, ROWS)
-    m_up = remote(m.at[2, body_rows], m.at[0, body_rows], halo_send.at[0], halo_recv.at[0], {"space": above})
-    m_down = remote(m.at[1, body_rows], m.at[3, body_rows], halo_send.at[1], halo_recv.at[1], {"space": below})
-    m_up.start()
-    m_down.start()
-    r_down = remote(r0.at[:, 0], r0h, halo_send.at[2], halo_recv.at[2], {"space": below})
-    y_up = remote(y0.at[:, 1, whole], y0h.at[:, 0, whole], halo_send.at[3], halo_recv.at[3], {"space": above})
-    r_down.start()
-    y_up.start()
+    has_above, has_below = s < spaces - 1, s > 0
+    up, down = {"space": above}, {"space": below}
+
+    def start_up(*copies):
+        @pl.when(has_above)
+        def _():
+            for copy in copies:
+                copy.start()
+
+    def start_down(*copies):
+        @pl.when(has_below)
+        def _():
+            for copy in copies:
+                copy.start()
+
+    m_up = remote(m.at[2, body_rows], m.at[0, body_rows], halo_send.at[0], halo_recv.at[0], up)
+    m_down = remote(m.at[1, body_rows], m.at[3, body_rows], halo_send.at[1], halo_recv.at[1], down)
+    r_down, y_up, y1_down = [], [], []
+    for i in range(CHUNKS):
+        part_rows = pl.ds(i * CHUNK, CHUNK)
+        r_down.append(
+            remote(r0.at[:, 0, part_rows], r0h.at[:, part_rows], halo_send.at[3 + i], halo_recv.at[3 + i], down)
+        )
+        y_up.append(
+            remote(
+                y0.at[:, 1, part_rows], y0h.at[:, 0, part_rows],
+                halo_send.at[3 + CHUNKS + i], halo_recv.at[3 + CHUNKS + i], up,
+            )
+        )
+        done = pl.ds(DONE[i], DONE[i + 1] - DONE[i])
+        y1_down.append(
+            remote(
+                y1.at[:, 0, done], y1h.at[:, done],
+                halo_send.at[3 + 2 * CHUNKS + i], halo_recv.at[3 + 2 * CHUNKS + i], down,
+            )
+        )
+    start_up(m_up, *y_up)
+    start_down(m_down, *r_down)
     loaded[5].wait()
-    f_down = remote(
-        fw.at[:, 0, whole], fw.at[:, 2, whole], halo_send.at[4], halo_recv.at[4], {"space": below}
-    )
-    f_down.start()
+    f_down = remote(fw.at[:, 0, whole], fw.at[:, 2, whole], halo_send.at[2], halo_recv.at[2], down)
+    start_down(f_down)
+
+    def cleared(ref):
+        def body(row):
+            ref[pl.ds(row, 32), :] = jnp.zeros((32, ROWS), F32)
+
+        over_rows(body, 32)
+
+    @pl.when(s == 0)
+    def _():
+        cleared(m.at[0, body_rows])
+        for c in range(3):
+            cleared(y0h.at[c, 0])
+
+    @pl.when(s == spaces - 1)
+    def _():
+        cleared(m.at[3, body_rows])
+        for c in range(3):
+            cleared(r0h.at[c])
+            cleared(fw.at[c, 2])
+            cleared(y1h.at[c])
+
+    def wait_from_below(*copies):
+        @pl.when(has_below)
+        def _():
+            for copy in copies:
+                copy.wait_recv()
+
+    def wait_from_above(*copies):
+        @pl.when(has_above)
+        def _():
+            for copy in copies:
+                copy.wait_recv()
 
     def modes(plane, row, n):
         return [plane_modes(ref[pl.ds(row, n), :], ref[pl.ds(row + 1, n), :]) for ref in plane]
@@ -253,20 +333,12 @@
 
     forward_stress(0, 32)
 
-    m_up.wait_recv()
-    m_down.wait_recv()
-    r_down.wait_recv()
-    y_up.wait_recv()
-
-    @pl.when(s == 0)
-    def _():
-        m[0, TILE : TILE + ROWS, :] = jnp.zeros((ROWS, ROWS), F32)
-
-    @pl.when(s == spaces - 1)
-    def _():
-        r0h[...] = jnp.zeros((3, ROWS, ROWS), F32)
-
-    def own_second(row, n=64):
+    wait_from_below(m_up)
+    wait_from_above(m_down)
+    pl.semaphore_wait(known1, len(next1))
+    tell(known2, next2)
+
+    def own_second(row, n=CHUNK):
         at = pl.ds(row, n)
         inverse = (1 - msk[0, at, :]).astype(F32) * inverse_diagonal(0, 1, row, n)
         inv[0, at, :] = inverse
@@ -274,8 +346,6 @@
         for c in range(3):
             y0[c, 0, at, :] = inverse * r0[c, 0, at, :]
             y0h[c, 1, at, :] = beyond * r0h[c, at, :]
-
-    over_rows(own_second, 64)
 
     def product(row, held, n=16):
         carried, norm, curve, next_norm = held
@@ -314,33 +384,38 @@
                 next_norm = next_norm + folded(force * image)
         return tuple(passed), norm, curve, next_norm
 
-    _, norm, curve, next_norm = over_rows(product, 16, ((zero,) * 6, zero, zero, zero))
-
-    y1_down = remote(y1.at[:, 0, whole], y1h.at[:, whole], halo_send.at[5], halo_recv.at[5], {"space": below})
-    y1_down.start()
-
-    def against_forward(planes, first, out, energy, n):
-        def body(row, held):
+    held = ((zero,) * 6, zero, zero, zero)
+    for i in range(CHUNKS):
+        wait_from_above(r_down[i])
+        wait_from_below(y_up[i])
+        over_rows(own_second, CHUNK, None, i * CHUNK, (i + 1) * CHUNK)
+        held = over_rows(product, STEP, held, DONE[i], DONE[i + 1])
+        start_down(y1_down[i])
+    _, norm, curve, next_norm = held
+    pl.semaphore_wait(known2, len(next2))
+    tell(known3, next3)
+
+    def against_forward(planes, out, n):
+        def body(row):
             all_modes = [modes(plane, row, n) for plane in planes]
             at = pl.ds(row, n)
-            for i in range(len(planes) - 1):
-                layer = first + i
-                e = strains(all_modes[i], all_modes[i + 1])
+            for layer in range(2):
+                e = strains(all_modes[layer], all_modes[layer + 1])
                 out[layer, at, :] = UNIT * dot(e, [ff[layer, j, at, :] for j in range(18)])
-                if energy:
-                    held = held + folded((UNIT * m[1 + layer, pl.ds(row + TILE, n), :]) * dot(e, stresses(e)))
-            return held
-
-        return lambda held: over_rows(body, n, held)
-
-    f_down.wait_recv()
-
-    @pl.when(s == spaces - 1)
-    def _():
-        fw[:, 2, 0:ROWS, :] = jnp.zeros((3, ROWS, ROWS), F32)
-
+
+        over_rows(body, n)
+
+    def energy_of(layer, n):
+        def body(row, held):
+            e = strains(modes(y1_planes[layer], row, n), modes(y1_planes[layer + 1], row, n))
+            return held + folded((UNIT * m[1 + layer, pl.ds(row + TILE, n), :]) * dot(e, stresses(e)))
+
+        return body
+
+    energy = over_rows(energy_of(0, 32), 32, zero)
+    wait_from_above(f_down)
     forward_stress(1, 32)
-    against_forward(y0_planes[1:4], 0, g0, False, 16)(zero)
+    against_forward(y0_planes[1:4], g0, 16)
 
     def exchange(src, dst, sems):
         copies = []
@@ -354,102 +429,111 @@
         return copies
 
     sent = exchange(g0, g0r, 0)
-    energy = against_forward(y1_planes[0:2], 0, g1, True, 32)(zero)
-    y1_down.wait_recv()
-
-    @pl.when(s == spaces - 1)
-    def _():
-        y1h[:, 0:ROWS, :] = jnp.zeros((3, ROWS, ROWS), F32)
-
-    energy = against_forward(y1_planes[1:3], 1, g1, True, 32)(energy)
-
-    part[0:1, :] = jnp.sum(norm, axis=0, keepdims=True)
-    part[1:2, :] = jnp.sum(curve, axis=0, keepdims=True)
-    part[2:3, :] = jnp.sum(next_norm, axis=0, keepdims=True)
-    part[3:4, :] = jnp.sum(energy, axis=0, keepdims=True)
-    part[4:8, :] = jnp.zeros((4, ROWS), F32)
+    for i in range(CHUNKS):
+        wait_from_above(y1_down[i])
+        first, last = DONE[i] - STEP, DONE[i + 1] - STEP
+        energy = over_rows(energy_of(1, STEP), STEP, energy, max(first, 0), ROWS if i == CHUNKS - 1 else last)
+
+    lane = lax.broadcasted_iota(jnp.int32, (1, ROWS), 1)
+    quarter = ROWS // 4
+    sums = [jnp.sum(jnp.sum(v, axis=0, keepdims=True), axis=1, keepdims=True) for v in (norm, curve, next_norm, energy)]
+    part[...] = jnp.where(
+        lane < 2 * quarter,
+        jnp.where(lane < quarter, sums[0], sums[1]),
+        jnp.where(lane < 3 * quarter, sums[2], sums[3]),
+    )
     for slot, peer in zip(stage1, peers1):
         copy = remote(part, r1.at[within], s1_send.at[slot], s1_recv.at[within], peer)
         copy.start()
         sent.append(copy)
+    r1[within] = part[...]
+    against_forward(y1_planes, g1, 16)
     sent += exchange(g1, g1r, 1)
-    r1[within] = part[...]
-
-    def arrived(dst, slots, sems, like):
-        for slot in slots:
-            remote(like, dst.at[slot], sems.at[slot], sems.at[slot], near[0]).wait_recv()
-
-    arrived(r1, stage1, s1_recv, part)
+
+    for slot in stage1:
+        remote(part, r1.at[slot], s1_send.at[slot], s1_recv.at[slot], up).wait_recv()
     total = r1[0]
     for i in range(1, group):
         total = total + r1[i]
     mid[...] = total
-    for slot, peer in zip(stage2, peers2):
-        copy = remote(mid, r2.at[outer], s2_send.at[slot], s2_recv.at[outer], peer)
+    pl.semaphore_wait(known3, len(next3))
+    for (i, j), peer in zip(stage2, peers2):
+        copy = remote(mid, r2.at[outer, load], s2_send.at[i, j], s2_recv.at[outer, load], peer)
         copy.start()
         sent.append(copy)
-    r2[outer] = total
-    arrived(r2, stage2, s2_recv, mid)
-    total = r2[0]
-    for i in range(1, wide):
-        total = total + r2[i]
-
-    sums = jnp.sum(total, axis=1, keepdims=True)
-    sums = jnp.broadcast_to(sums, (TILE, ROWS))
-    rr, rq, qq, qd = sums[0:1], sums[1:2], sums[2:3], sums[3:4]
-    step = rr / rq
-    norm_next = step * (step * qq) - rr
-    ratio = norm_next / rr
-    curve_next = rq - 2.0 * (step * qq) + step * (step * qd)
-    step_next = norm_next / (curve_next - ratio * norm_next / step)
-    first = step + step_next * (1.0 + ratio)
-    second = -(step_next * step)
-    coef[...] = jnp.concatenate([first, second, jnp.zeros((6, ROWS), F32)], axis=0)
-    for slot, peer in zip(stage3, peers3):
-        copy = remote(coef, r3.at[load], s3_send.at[slot], s3_recv.at[load], peer)
-        copy.start()
-        sent.append(copy)
-    r3[load] = coef[...]
+    r2[outer, load] = total
+
+    def arrived(slots):
+        for i, j in slots:
+            remote(mid, r2.at[i, j], s2_send.at[i, j], s2_recv.at[i, j], up).wait_recv()
+
+    def coefficients(sums):
+        rr, rq, qq, qd = [sums[:, i * quarter : i * quarter + 1] for i in range(4)]
+        step = rr / rq
+        norm_next = step * (step * qq) - rr
+        ratio = norm_next / rr
+        curve_next = rq - 2.0 * (step * qq) + step * (step * qd)
+        step_next = norm_next / (curve_next - ratio * norm_next / step)
+        return step + step_next * (1.0 + ratio), -(step_next * step)
+
+    def summed(j):
+        total = r2[0, j]
+        for i in range(1, wide):
+            total = total + r2[i, j]
+        return total
+
+    arrived(stage2[loads * 1 - 1 :: loads])
+    first, second = coefficients(summed(load))
+
+    def solve(row, n=32):
+        at = pl.ds(row, n)
+        for c in range(3):
+            for plane in range(2):
+                x_out[c, plane, at, :] = first * y0[c, plane, at, :] + second * y1[c, plane, at, :]
+
+    over_rows(solve, 32)
 
     mine = pl.ds(pl.multiple_of(load * rows, rows), rows)
     g0r[load] = g0[:, mine, :]
     g1r[load] = g1[:, mine, :]
-    scale_out[...] = sc[:, mine, :]
     for slot in stage3:
-        remote(g0.at[:, pl.ds(0, rows)], g0r.at[slot], z_send.at[0, slot], z_recv.at[0, slot], near[0]).wait_recv()
-        remote(g1.at[:, pl.ds(0, rows)], g1r.at[slot], z_send.at[1, slot], z_recv.at[1, slot], near[0]).wait_recv()
-    arrived(r3, stage3, s3_recv, coef)
+        remote(g0.at[:, pl.ds(0, rows)], g0r.at[slot], z_send.at[0, slot], z_recv.at[0, slot], up).wait_recv()
+        remote(g1.at[:, pl.ds(0, rows)], g1r.at[slot], z_send.at[1, slot], z_recv.at[1, slot], up).wait_recv()
+    arrived([(i, j) for k, (i, j) in enumerate(stage2) if (k + 1) % loads])
+    first, second = coefficients(jnp.concatenate([summed(j) for j in range(loads)], axis=0))
+    coefs[0] = jnp.broadcast_to(first, (loads, ROWS))
+    coefs[1] = jnp.broadcast_to(second, (loads, ROWS))
     total = None
     for i in range(loads):
-        term = r3[i, 0:1, :][None] * g0r[i] + r3[i, 1:2, :][None] * g1r[i]
+        term = coefs[0, i : i + 1, :][None] * g0r[i] + coefs[1, i : i + 1, :][None] * g1r[i]
         total = term if total is None else total + term
-    gsum[...] = total
-
-    for copy in (m_up, m_down, r_down, y_up, f_down, y1_down):
-        copy.wait_send()
+    grad_out[...] = sc[:, mine, :] * total
+
+    @pl.when(has_above)
+    def _():
+        for copy in (m_up, *y_up):
+            copy.wait_send()
+
+    @pl.when(has_below)
+    def _():
+        for copy in (m_down, f_down, *r_down, *y1_down):
+            copy.wait_send()
+
     for copy in sent:
         copy.wait_send()
 
 
-def finish(y0, y1, coef, gsum, scale, x_out, grad_out, x, grad, sem):
-    grad[...] = scale[...] * gsum[...]
-    copies = [pltpu.make_async_copy(grad, grad_out, sem.at[3])]
-    copies[0].start()
-    first = jnp.broadcast_to(coef[0:1, :], (ROWS, ROWS))
-    second = jnp.broadcast_to(coef[1:2, :], (ROWS, ROWS))
-    for c in range(3):
-        for plane in range(2):
-            x[c, plane] = first * y0[c, plane, 0:ROWS, :] + second * y1[c, plane, 0:ROWS, :]
-        copy = pltpu.make_async_copy(x.at[c], x_out.at[0, c], sem.at[c])
+def finish(x, grad, x_out, grad_out, sem):
+    copies = [pltpu.make_async_copy(x, x_out.at[0], sem.at[0]), pltpu.make_async_copy(grad, grad_out, sem.at[1])]
+    for copy in copies:
         copy.start()
-        copies.append(copy)
     for copy in copies:
         copy.wait()
 
 
 def solution(mesh):
     spaces, loads = mesh.shape["space"], mesh.shape["load"]
-    group = 16
+    group = 2 * LONG
     rows = ROWS // loads
 
     def shards(forward_disp, adjoint_rhs, modulus_factor, zone_base, zone_ids, fixed_mask):
@@ -465,35 +549,33 @@
             pltpu.with_memory_space_constraint(a, pltpu.HBM)
             for a in (forward_disp, adjoint_rhs, modulus_factor, zone_base, zone_ids, fixed_mask)
         ]
-        y0, y1, coef, gsum, scale = pl.pallas_call(
+        x, grad = pl.pallas_call(
             functools.partial(kernel, spaces=spaces, loads=loads, group=group),
-            out_shape=(
-                out(3, 2, *padded), out(3, 2, *padded), out(TILE, ROWS), out(2, rows, ROWS), out(2, rows, ROWS)
-            ),
+            out_shape=(out(3, 2, *plane), out(2, rows, ROWS)),
             in_specs=[hbm] * 6,
-            out_specs=(held,) * 5,
+            out_specs=(held,) * 2,
             scratch_shapes=[
                 pltpu.SMEM(zone_base.shape, F32),
                 vmem(2, *plane), ints(2, *plane), ints(2, *plane), vmem(3, 2, *plane), vmem(3, 3, *padded),
-                vmem(2, *plane), vmem(4, *padded), vmem(3, 2, *padded), vmem(3, *padded),
+                vmem(2, *plane), vmem(4, *padded), vmem(3, 2, *padded), vmem(3, 2, *padded), vmem(3, 2, *padded), vmem(3, *padded),
                 vmem(2, *plane), vmem(3, 2, *plane), vmem(3, *plane), vmem(2, 18, *plane),
                 vmem(2, *plane), vmem(2, *plane), vmem(loads, 2, rows, ROWS), vmem(loads, 2, rows, ROWS),
-                vmem(TILE, ROWS), vmem(group, TILE, ROWS), vmem(TILE, ROWS), vmem(spaces // group, TILE, ROWS),
-                vmem(loads, TILE, ROWS),
-                dma((6,)), dma((6,)), dma((6,)), dma((2, loads)), dma((2, loads)),
-                dma((group,)), dma((group,)), dma((spaces // group,)), dma((spaces // group,)),
-                dma((loads,)), dma((loads,)),
+                vmem(1, ROWS), vmem(group, 1, ROWS), vmem(1, ROWS), vmem(spaces // group, loads, 1, ROWS),
+                vmem(2, loads, ROWS),
+                dma((6,)), dma((3 + 3 * CHUNKS,)), dma((3 + 3 * CHUNKS,)), dma((2, loads)), dma((2, loads)),
+                dma((group,)), dma((group,)), dma((spaces // group, loads)), dma((spaces // group, loads)),
+                *[pltpu.SemaphoreType.REGULAR] * 3,
             ],
             compiler_params=pltpu.CompilerParams(collective_id=0, has_side_effects=True, vmem_limit_bytes=LIMIT),
         )(*pinned)
         return pl.pallas_call(
             finish,
             out_shape=(out(1, 3, 2, *plane), out(2, rows, ROWS)),
-            in_specs=[held] * 5,
+            in_specs=[held] * 2,
             out_specs=(hbm, hbm),
-            scratch_shapes=[vmem(3, 2, *plane), vmem(2, rows, ROWS), dma((4,))],
+            scratch_shapes=[dma((2,))],
             compiler_params=pltpu.CompilerParams(vmem_limit_bytes=4 * 2**20),
-        )(y0, y1, coef, gsum, scale)
+        )(x, grad)
 
     placed = (
         P("load", None, "space", None, None),

time: 42.4 us -> 36.6 us (0.86); the launches traced: 41.7 us -> 36.4 us
  Pallas kernels: 41.1 us -> 35.8 us
    pallas_call x1, Pallas kernels: 40.3 us -> 35 us  [shards(): pl.pallas_call(functools.partial(kernel, spaces=spaces, loads=loads, grou...]
where the time goes in v3:
time: 36.6 us; the launch traced here: 36.4 us
  Pallas kernels  35.8 us (98%)
  between operations  0.64 us (2%)
    pallas_call x1, Pallas kernels, shards(): pl.pallas_call(functools.partial(kernel, spaces=spaces, loads=loads, grou...  35 us
    pallas_call x1, Pallas kernels, shards(): pl.pallas_call(finish, out_shape=(out(1, 3, 2, *plane), out(2, rows, ROWS...  0.77 us

profile of v3, /device:TPU:1, one launch (start us, length us, event | category | flops | bytes accessed | tf_op | source)
XLA Modules:
  0.0 36.4 jit_solution(12493239853707614530)
XLA Ops:
  0.6 35.0 %shard_map.77 = (f32[3,2,128,128]{3,2,1,0:T(8,128)S(1)}, f32[2,16,128]{2,1,0:T(8,128)S(1)}) custom-call(f32[1,3,2,128,128]{4,3,2,1,0:T(8,128)} %fwd_hbm.1, f32[1,3,2,128,128]{4,3,2,1,0:T(8,128)} %rhs_hbm.1, f32[2,128,128]{2,1,0:T(8,128)} %fac_hbm.1, f32[8]{0:T(128)} %base_hbm.1, s32[2,128,128]{2,1,0:T(8,128)} %ids_hbm.1, s32[2,128,128]{2,1,0:T(8,128)} %msk_hbm.1), custom_call_target="tpu_custom_call" | custom-call | tf_op jit(solution)/shard_map/pallas_call | solution.py:552
  35.7 0.8 %shard_map.78 = (f32[1,3,2,128,128]{4,3,2,1,0:T(8,128)}, f32[2,16,128]{2,1,0:T(8,128)}) custom-call(f32[3,2,128,128]{3,2,1,0:T(8,128)S(1)} %get-tuple-element.4.x, f32[2,16,128]{2,1,0:T(8,128)S(1)} %get-tuple-element.5.grad), custom_call_target="tpu_custom_call" | custom-call | tf_op jit(solution)/shard_map/pallas_call | solution.py:571

commit v4 on v3

--- a/solution.py
+++ b/solution.py
@@ -121,10 +121,10 @@
 
 def kernel(
     fwd_hbm, rhs_hbm, fac_hbm, base_hbm, ids_hbm, msk_hbm,
-    x_out, grad_out,
-    base, fac, ids, msk, rhs, fw, sc, m, y0, y1, y0h, y1h, inv, r0, r0h, ff, g0, g1, g0r, g1r,
+    x_hbm, grad_hbm,
+    x_out, grad_out, base, fac, ids, msk, rhs, fw, sc, m, y0, y1, y0h, y1h, inv, r0, r0h, ff, g0, g1, gr,
     part, r1, mid, r2, coefs,
-    load_sem, halo_send, halo_recv, z_send, z_recv, s1_send, s1_recv, s2_send, s2_recv, known1, known2, known3,
+    load_sem, halo_send, halo_recv, sum_send, sum_recv, known1, known2, known3,
     *, spaces, loads, group,
 ):
     s = lax.axis_index("space")
@@ -168,8 +168,9 @@
 
     stage1 = [lax.rem(within + i, group) for i in range(1, group)]
     peers1 = [{"space": outer * group + i} for i in stage1]
-    stage2 = [(lax.rem(outer + i, wide), lax.rem(load + j, loads)) for i in range(wide) for j in range(loads)][1:]
-    peers2 = [{"space": i * group + within, "load": j} for i, j in stage2]
+    stage2 = [lax.rem(outer + i, wide) * group + within for i in range(wide)]
+    peers_own = [{"space": i} for i in stage2[1:]]
+    peers_other = [{"space": i, "load": lax.rem(load + j, loads)} for i in stage2 for j in range(1, loads)]
     stage3 = [lax.rem(load + i, loads) for i in range(1, loads)]
     peers3 = [{"load": i} for i in stage3]
 
@@ -254,25 +255,25 @@
     for i in range(CHUNKS):
         part_rows = pl.ds(i * CHUNK, CHUNK)
         r_down.append(
-            remote(r0.at[:, 0, part_rows], r0h.at[:, part_rows], halo_send.at[3 + i], halo_recv.at[3 + i], down)
+            remote(r0.at[:, 0, part_rows], r0h.at[:, part_rows], halo_send.at[1], halo_recv.at[3 + i], down)
         )
         y_up.append(
             remote(
                 y0.at[:, 1, part_rows], y0h.at[:, 0, part_rows],
-                halo_send.at[3 + CHUNKS + i], halo_recv.at[3 + CHUNKS + i], up,
+                halo_send.at[0], halo_recv.at[3 + CHUNKS + i], up,
             )
         )
         done = pl.ds(DONE[i], DONE[i + 1] - DONE[i])
         y1_down.append(
             remote(
                 y1.at[:, 0, done], y1h.at[:, done],
-                halo_send.at[3 + 2 * CHUNKS + i], halo_recv.at[3 + 2 * CHUNKS + i], down,
+                halo_send.at[1], halo_recv.at[3 + 2 * CHUNKS + i], down,
             )
         )
     start_up(m_up, *y_up)
     start_down(m_down, *r_down)
     loaded[5].wait()
-    f_down = remote(fw.at[:, 0, whole], fw.at[:, 2, whole], halo_send.at[2], halo_recv.at[2], down)
+    f_down = remote(fw.at[:, 0, whole], fw.at[:, 2, whole], halo_send.at[1], halo_recv.at[2], down)
     start_down(f_down)
 
     def cleared(ref):
@@ -417,18 +418,17 @@
     forward_stress(1, 32)
     against_forward(y0_planes[1:4], g0, 16)
 
-    def exchange(src, dst, sems):
-        copies = []
+    def taken(sem, ref):
+        pltpu.make_async_copy(ref, ref, sem).wait()
+
+    def exchange(src, slots):
         for slot, peer in zip(stage3, peers3):
-            copy = remote(
-                src.at[:, pl.ds(pl.multiple_of(slot * rows, rows), rows)], dst.at[load],
-                z_send.at[sems, slot], z_recv.at[sems, load], peer,
-            )
-            copy.start()
-            copies.append(copy)
-        return copies
-
-    sent = exchange(g0, g0r, 0)
+            remote(
+                src.at[:, pl.ds(pl.multiple_of(slot * rows, rows), rows)], gr.at[slots + load],
+                sum_send.at[0], sum_recv.at[0], peer,
+            ).start()
+
+    exchange(g0, 0)
     for i in range(CHUNKS):
         wait_from_above(y1_down[i])
         first, last = DONE[i] - STEP, DONE[i + 1] - STEP
@@ -442,30 +442,23 @@
         jnp.where(lane < quarter, sums[0], sums[1]),
         jnp.where(lane < 3 * quarter, sums[2], sums[3]),
     )
-    for slot, peer in zip(stage1, peers1):
-        copy = remote(part, r1.at[within], s1_send.at[slot], s1_recv.at[within], peer)
-        copy.start()
-        sent.append(copy)
+    for peer in peers1:
+        remote(part, r1.at[within], sum_send.at[1], sum_recv.at[1], peer).start()
     r1[within] = part[...]
     against_forward(y1_planes, g1, 16)
-    sent += exchange(g1, g1r, 1)
-
-    for slot in stage1:
-        remote(part, r1.at[slot], s1_send.at[slot], s1_recv.at[slot], up).wait_recv()
+    exchange(g1, loads)
+
+    taken(sum_recv.at[1], r1.at[pl.ds(0, group - 1)])
     total = r1[0]
     for i in range(1, group):
         total = total + r1[i]
     mid[...] = total
     pl.semaphore_wait(known3, len(next3))
-    for (i, j), peer in zip(stage2, peers2):
-        copy = remote(mid, r2.at[outer, load], s2_send.at[i, j], s2_recv.at[outer, load], peer)
-        copy.start()
-        sent.append(copy)
+    for peer in peers_own:
+        remote(mid, r2.at[outer, load], sum_send.at[2], sum_recv.at[2], peer).start()
+    for peer in peers_other:
+        remote(mid, r2.at[outer, load], sum_send.at[3], sum_recv.at[3], peer).start()
     r2[outer, load] = total
-
-    def arrived(slots):
-        for i, j in slots:
-            remote(mid, r2.at[i, j], s2_send.at[i, j], s2_recv.at[i, j], up).wait_recv()
 
     def coefficients(sums):
         rr, rq, qq, qd = [sums[:, i * quarter : i * quarter + 1] for i in range(4)]
@@ -482,7 +475,7 @@
             total = total + r2[i, j]
         return total
 
-    arrived(stage2[loads * 1 - 1 :: loads])
+    taken(sum_recv.at[2], r2.at[pl.ds(0, wide - 1), 0])
     first, second = coefficients(summed(load))
 
     def solve(row, n=32):
@@ -492,35 +485,41 @@
                 x_out[c, plane, at, :] = first * y0[c, plane, at, :] + second * y1[c, plane, at, :]
 
     over_rows(solve, 32)
+    x_copy = pltpu.make_async_copy(x_out, x_hbm, load_sem.at[0])
+    x_copy.start()
 
     mine = pl.ds(pl.multiple_of(load * rows, rows), rows)
-    g0r[load] = g0[:, mine, :]
-    g1r[load] = g1[:, mine, :]
-    for slot in stage3:
-        remote(g0.at[:, pl.ds(0, rows)], g0r.at[slot], z_send.at[0, slot], z_recv.at[0, slot], up).wait_recv()
-        remote(g1.at[:, pl.ds(0, rows)], g1r.at[slot], z_send.at[1, slot], z_recv.at[1, slot], up).wait_recv()
-    arrived([(i, j) for k, (i, j) in enumerate(stage2) if (k + 1) % loads])
+    gr[load] = g0[:, mine, :]
+    gr[loads + load] = g1[:, mine, :]
+    taken(sum_recv.at[0], gr.at[pl.ds(0, 2 * (loads - 1))])
+
+    taken(sum_send.at[0], gr.at[pl.ds(0, 2 * (loads - 1))])
+    taken(sum_send.at[1], r1.at[pl.ds(0, group - 1)])
+
+    @pl.when(has_above)
+    def _():
+        taken(halo_send.at[0], ff.at[0, pl.ds(0, 4)])
+
+    @pl.when(has_below)
+    def _():
+        taken(halo_send.at[1], ff.at[0, pl.ds(0, 10)])
+
+    taken(sum_recv.at[3], r2.at[pl.ds(0, wide), pl.ds(0, loads - 1)])
     first, second = coefficients(jnp.concatenate([summed(j) for j in range(loads)], axis=0))
     coefs[0] = jnp.broadcast_to(first, (loads, ROWS))
     coefs[1] = jnp.broadcast_to(second, (loads, ROWS))
     total = None
     for i in range(loads):
-        term = coefs[0, i : i + 1, :][None] * g0r[i] + coefs[1, i : i + 1, :][None] * g1r[i]
+        term = coefs[0, i : i + 1, :][None] * gr[i] + coefs[1, i : i + 1, :][None] * gr[loads + i]
         total = term if total is None else total + term
     grad_out[...] = sc[:, mine, :] * total
-
-    @pl.when(has_above)
-    def _():
-        for copy in (m_up, *y_up):
-            copy.wait_send()
-
-    @pl.when(has_below)
-    def _():
-        for copy in (m_down, f_down, *r_down, *y1_down):
-            copy.wait_send()
-
-    for copy in sent:
-        copy.wait_send()
+    grad_copy = pltpu.make_async_copy(grad_out, grad_hbm, load_sem.at[1])
+    grad_copy.start()
+
+    taken(sum_send.at[3], r2.at[pl.ds(0, wide), pl.ds(0, loads - 1)])
+    taken(sum_send.at[2], r2.at[pl.ds(0, wide - 1), 0])
+    x_copy.wait()
+    grad_copy.wait()
 
 
 def finish(x, grad, x_out, grad_out, sem):
@@ -543,7 +542,7 @@
         ints = lambda *shape: pltpu.VMEM(shape, jnp.int32)
         dma = pltpu.SemaphoreType.DMA
         hbm = pl.BlockSpec(memory_space=pltpu.HBM)
-        held = pl.BlockSpec(memory_space=pltpu.VMEM)
+        anywhere = pl.BlockSpec(memory_space=pl.ANY)
         out = lambda *shape: jax.ShapeDtypeStruct(shape, F32)
         pinned = [
             pltpu.with_memory_space_constraint(a, pltpu.HBM)
@@ -553,17 +552,16 @@
             functools.partial(kernel, spaces=spaces, loads=loads, group=group),
             out_shape=(out(3, 2, *plane), out(2, rows, ROWS)),
             in_specs=[hbm] * 6,
-            out_specs=(held,) * 2,
+            out_specs=(anywhere,) * 2,
             scratch_shapes=[
-                pltpu.SMEM(zone_base.shape, F32),
+                vmem(3, 2, *plane), vmem(2, rows, ROWS), pltpu.SMEM(zone_base.shape, F32),
                 vmem(2, *plane), ints(2, *plane), ints(2, *plane), vmem(3, 2, *plane), vmem(3, 3, *padded),
                 vmem(2, *plane), vmem(4, *padded), vmem(3, 2, *padded), vmem(3, 2, *padded), vmem(3, 2, *padded), vmem(3, *padded),
                 vmem(2, *plane), vmem(3, 2, *plane), vmem(3, *plane), vmem(2, 18, *plane),
-                vmem(2, *plane), vmem(2, *plane), vmem(loads, 2, rows, ROWS), vmem(loads, 2, rows, ROWS),
+                vmem(2, *plane), vmem(2, *plane), vmem(2 * loads, 2, rows, ROWS),
                 vmem(1, ROWS), vmem(group, 1, ROWS), vmem(1, ROWS), vmem(spaces // group, loads, 1, ROWS),
                 vmem(2, loads, ROWS),
-                dma((6,)), dma((3 + 3 * CHUNKS,)), dma((3 + 3 * CHUNKS,)), dma((2, loads)), dma((2, loads)),
-                dma((group,)), dma((group,)), dma((spaces // group, loads)), dma((spaces // group, loads)),
+                dma((6,)), dma((2,)), dma((3 + 3 * CHUNKS,)), dma((4,)), dma((4,)),
                 *[pltpu.SemaphoreType.REGULAR] * 3,
             ],
             compiler_params=pltpu.CompilerParams(collective_id=0, has_side_effects=True, vmem_limit_bytes=LIMIT),
@@ -571,7 +569,7 @@
         return pl.pallas_call(
             finish,
             out_shape=(out(1, 3, 2, *plane), out(2, rows, ROWS)),
-            in_specs=[held] * 2,
+            in_specs=[anywhere] * 2,
             out_specs=(hbm, hbm),
             scratch_shapes=[dma((2,))],
             compiler_params=pltpu.CompilerParams(vmem_limit_bytes=4 * 2**20),

time: 36.6 us -> 35.3 us (0.964)
  Pallas kernels: 35.8 us -> 34.5 us
    pallas_call x1, Pallas kernels: 35 us -> 33.7 us  [shards(): pl.pallas_call(functools.partial(kernel, spaces=spaces, loads=loads, grou...]
where the time goes in v4:
time: 35.3 us; the launch traced here: 35.1 us
  Pallas kernels  34.5 us (98%)
  between operations  0.64 us (2%)
    pallas_call x1, Pallas kernels, shards(): pl.pallas_call(functools.partial(kernel, spaces=spaces, loads=loads, grou...  33.7 us
    pallas_call x1, Pallas kernels, shards(): pl.pallas_call(finish, out_shape=(out(1, 3, 2, *plane), out(2, rows, ROWS...  0.77 us

profile of v4, /device:TPU:1, one launch (start us, length us, event | category | flops | bytes accessed | tf_op | source)
XLA Modules:
  0.0 35.1 jit_solution(9862729930267314586)
XLA Ops:
  0.6 33.7 %shard_map.77 = (f32[3,2,128,128]{3,2,1,0:T(8,128)S(1)}, f32[2,16,128]{2,1,0:T(8,128)S(1)}) custom-call(f32[1,3,2,128,128]{4,3,2,1,0:T(8,128)} %fwd_hbm.1, f32[1,3,2,128,128]{4,3,2,1,0:T(8,128)} %rhs_hbm.1, f32[2,128,128]{2,1,0:T(8,128)} %fac_hbm.1, f32[8]{0:T(128)} %base_hbm.1, s32[2,128,128]{2,1,0:T(8,128)} %ids_hbm.1, s32[2,128,128]{2,1,0:T(8,128)} %msk_hbm.1), custom_call_target="tpu_custom_call" | custom-call | tf_op jit(solution)/shard_map/pallas_call | solution.py:551
  34.4 0.8 %shard_map.78 = (f32[1,3,2,128,128]{4,3,2,1,0:T(8,128)}, f32[2,16,128]{2,1,0:T(8,128)}) custom-call(f32[3,2,128,128]{3,2,1,0:T(8,128)S(1)} %get-tuple-element.4.x, f32[2,16,128]{2,1,0:T(8,128)S(1)} %get-tuple-element.5.grad), custom_call_target="tpu_custom_call" | custom-call | tf_op jit(solution)/shard_map/pallas_call | solution.py:569

commit v5 on v4

--- a/solution.py
+++ b/solution.py
@@ -14,9 +14,9 @@
 TILE = 8
 LONG = 8
 STEP = 16
-CHUNKS = 4
-CHUNK = ROWS // CHUNKS
-DONE = [0] + [(i + 1) * CHUNK - STEP for i in range(CHUNKS - 1)] + [ROWS]
+CUTS = [0, 32, 64, 96, 112, ROWS]
+CHUNKS = len(CUTS) - 1
+DONE = [0] + [cut - STEP for cut in CUTS[1:-1]] + [ROWS]
 LIMIT = 40 * 2**20
 
 POISSON = 0.3
@@ -36,10 +36,13 @@
     return jnp.where(first, 0.0, pltpu.roll(value, 1, 1))
 
 
-def plane_modes(here, after):
-    total, slope = here + after, after - here
-    total_next, slope_next = shifted_down(total), shifted_down(slope)
-    return (total + total_next, total_next - total, slope + slope_next, slope_next - slope)
+def plane_modes(pairs, row, n):
+    out = []
+    for sums, slopes in pairs:
+        here, after = sums[pl.ds(row, n), :], sums[pl.ds(row + 1, n), :]
+        slope, slope_after = slopes[pl.ds(row, n), :], slopes[pl.ds(row + 1, n), :]
+        out.append((here + after, slope + slope_after, after - here, slope_after - slope))
+    return out
 
 
 def strains(low, high):
@@ -64,18 +67,22 @@
     )
 
 
-def stresses(e):
-    trace = KAPPA * (e[0] + e[1] + e[2])
-    out = [2.0 * e[0] + trace, 2.0 * e[1] + trace, 2.0 * e[2] + trace, e[3], e[4], e[5]]
-    own, cross = 1.0, KAPPA / 3.0
+def stresses(e, modulus=None):
+    third, last = 1.0 / 3.0, (KAPPA + 4.0) / 9.0
+    if modulus is None:
+        two = 2.0
+        times = lambda value: value
+    else:
+        two, third, last = 2.0 * modulus, third * modulus, last * modulus
+        times = lambda value: modulus * value
+    half = (0.5 * KAPPA) * (e[0] + e[1] + e[2])
+    out = [two * (e[0] + half), two * (e[1] + half), two * (e[2] + half), times(e[3]), times(e[4]), times(e[5])]
     for a, b in ((6, 7), (8, 9), (10, 11)):
-        both = cross * (e[a] + e[b])
-        out += [own * e[a] + both, own * e[b] + both]
-    third = 1.0 / 3.0
-    shear = (e[12] + e[13] + e[14]) * third
-    out += [e[12] * third + shear, e[13] * third + shear, e[14] * third + shear]
-    last = (KAPPA + 4.0) / 9.0
-    out += [e[15] * last, e[16] * last, e[17] * last]
+        both = (KAPPA / 3.0) * (e[a] + e[b])
+        out += [times(e[a] + both), times(e[b] + both)]
+    shear = e[12] + e[13] + e[14]
+    out += [third * (e[12] + shear), third * (e[13] + shear), third * (e[14] + shear)]
+    out += [last * e[15], last * e[16], last * e[17]]
     return out
 
 
@@ -87,12 +94,13 @@
     )
 
 
-def onto_lower(g):
-    return (-g[2], g[0] - g[4], g[1] - g[5], g[3] - g[6])
-
-
-def onto_upper(g):
-    return (g[2], g[0] + g[4], g[1] + g[5], g[3] + g[6])
+def onto_plane(under, over):
+    return (
+        under[2] - over[2],
+        (under[0] + under[4]) + (over[0] - over[4]),
+        (under[1] + under[5]) + (over[1] - over[5]),
+        (under[3] + under[6]) + (over[3] - over[6]),
+    )
 
 
 def dot(a, b):
@@ -122,7 +130,7 @@
 def kernel(
     fwd_hbm, rhs_hbm, fac_hbm, base_hbm, ids_hbm, msk_hbm,
     x_hbm, grad_hbm,
-    x_out, grad_out, base, fac, ids, msk, rhs, fw, sc, m, y0, y1, y0h, y1h, inv, r0, r0h, ff, g0, g1, gr,
+    x_out, grad_out, base, fac, ids, msk, rhs, fw, sc, m, y0, y1, y0h, y1h, y0x, y1x, fwx, passed, inv, r0, r0h, ff, g0, g1, gr,
     part, r1, mid, r2, coefs,
     load_sem, halo_send, halo_recv, sum_send, sum_recv, known1, known2, known3,
     *, spaces, loads, group,
@@ -143,7 +151,7 @@
         local(ids_hbm, ids, 1),
         local(msk_hbm, msk, 2),
         local(rhs_hbm.at[0], rhs, 3),
-        local(fwd_hbm.at[0, :, pl.ds(0, 2)], fw.at[:, pl.ds(0, 2), pl.ds(0, ROWS)], 4),
+        local(fwd_hbm.at[0], fw.at[:, pl.ds(0, 2)], 4),
     ]
     for copy in loaded:
         copy.start()
@@ -166,12 +174,17 @@
     barrier = pltpu.get_barrier_semaphore()
     tell(barrier, near)
 
-    stage1 = [lax.rem(within + i, group) for i in range(1, group)]
+    far = lambda step, size: min(step, size - step)
+    order1 = sorted(range(1, group), key=lambda i: -far(i // 2 + i % 2, LONG))
+    order2 = sorted(
+        ((i, j) for i in range(wide) for j in range(1, loads)), key=lambda ij: -far(ij[0], wide) - far(ij[1], loads)
+    )
+    stage1 = [lax.rem(within + i, group) for i in order1]
     peers1 = [{"space": outer * group + i} for i in stage1]
     stage2 = [lax.rem(outer + i, wide) * group + within for i in range(wide)]
     peers_own = [{"space": i} for i in stage2[1:]]
-    peers_other = [{"space": i, "load": lax.rem(load + j, loads)} for i in stage2 for j in range(1, loads)]
-    stage3 = [lax.rem(load + i, loads) for i in range(1, loads)]
+    peers_other = [{"space": stage2[i], "load": lax.rem(load + j, loads)} for i, j in order2]
+    stage3 = [lax.rem(load + i, loads) for i in sorted(range(1, loads), key=lambda i: -far(i, loads))]
     peers3 = [{"load": i} for i in stage3]
 
     def remote(src, dst, send, recv, device):
@@ -184,13 +197,13 @@
     for layer in range(4):
         m[layer, 0:TILE, :] = zero
     for c in range(3):
-        y1h[c, past, :] = zero
-        for plane in range(2):
-            y0[c, plane, past, :] = zero
-            y0h[c, plane, past, :] = zero
-            y1[c, plane, past, :] = zero
-        for plane in range(3):
-            fw[c, plane, past, :] = zero
+        for k in range(2):
+            passed[2 * c + k, 0:TILE, :] = zero
+            for plane in range(3):
+                y1x[plane, c, k, past, :] = zero
+                fwx[plane, c, k, past, :] = zero
+            for plane in range(4):
+                y0x[plane, c, k, past, :] = zero
 
     for copy in loaded[:3]:
         copy.wait()
@@ -203,10 +216,34 @@
             scale = jnp.full((n, ROWS), bases[0], F32)
             for i in range(1, len(bases)):
                 scale = jnp.where(zone == i, bases[i], scale)
+            scale = UNIT * scale
             sc[layer, at, :] = scale
             m[1 + layer, pl.ds(row + TILE, n), :] = fac[layer, at, :] * scale
 
     over_rows(moduli, 16)
+    pl.semaphore_wait(barrier, len(near))
+    body_rows = pl.ds(TILE, ROWS)
+    has_above, has_below = s < spaces - 1, s > 0
+    up, down = {"space": above}, {"space": below}
+
+    def start_up(*copies):
+        @pl.when(has_above)
+        def _():
+            for copy in copies:
+                copy.start()
+
+    def start_down(*copies):
+        @pl.when(has_below)
+        def _():
+            for copy in copies:
+                copy.start()
+
+    m_up = remote(m.at[2, body_rows], m.at[0, body_rows], halo_send.at[0], halo_recv.at[0], up)
+    m_down = remote(m.at[1, body_rows], m.at[3, body_rows], halo_send.at[1], halo_recv.at[1], down)
+    start_up(m_up)
+    start_down(m_down)
+    tell(known1, next1)
+
     loaded[3].wait()
     loaded[4].wait()
 
@@ -214,7 +251,7 @@
         here = m[low, pl.ds(row + TILE, n), :] + m[high, pl.ds(row + TILE, n), :]
         before = m[low, pl.ds(row + TILE - 1, n), :] + m[high, pl.ds(row + TILE - 1, n), :]
         total = here + before
-        return 1.0 / (DIAG * (total + shifted_up(total)))
+        return 1.0 / ((DIAG / UNIT) * (total + shifted_up(total)))
 
     def own_first(row, n=64):
         at = pl.ds(row, n)
@@ -230,36 +267,15 @@
 
     over_rows(own_first, 64)
 
-    pl.semaphore_wait(barrier, len(near))
-    tell(known1, next1)
-    body_rows = pl.ds(TILE, ROWS)
-    whole = pl.ds(0, ROWS)
-    has_above, has_below = s < spaces - 1, s > 0
-    up, down = {"space": above}, {"space": below}
-
-    def start_up(*copies):
-        @pl.when(has_above)
-        def _():
-            for copy in copies:
-                copy.start()
-
-    def start_down(*copies):
-        @pl.when(has_below)
-        def _():
-            for copy in copies:
-                copy.start()
-
-    m_up = remote(m.at[2, body_rows], m.at[0, body_rows], halo_send.at[0], halo_recv.at[0], up)
-    m_down = remote(m.at[1, body_rows], m.at[3, body_rows], halo_send.at[1], halo_recv.at[1], down)
     r_down, y_up, y1_down = [], [], []
     for i in range(CHUNKS):
-        part_rows = pl.ds(i * CHUNK, CHUNK)
+        part_rows = pl.ds(CUTS[i], CUTS[i + 1] - CUTS[i])
         r_down.append(
             remote(r0.at[:, 0, part_rows], r0h.at[:, part_rows], halo_send.at[1], halo_recv.at[3 + i], down)
         )
         y_up.append(
             remote(
-                y0.at[:, 1, part_rows], y0h.at[:, 0, part_rows],
+                y0.at[:, 1, part_rows], y0h.at[:, part_rows],
                 halo_send.at[0], halo_recv.at[3 + CHUNKS + i], up,
             )
         )
@@ -270,10 +286,10 @@
                 halo_send.at[1], halo_recv.at[3 + 2 * CHUNKS + i], down,
             )
         )
-    start_up(m_up, *y_up)
-    start_down(m_down, *r_down)
+    start_down(*r_down)
+    start_up(*y_up)
     loaded[5].wait()
-    f_down = remote(fw.at[:, 0, whole], fw.at[:, 2, whole], halo_send.at[1], halo_recv.at[2], down)
+    f_down = remote(fw.at[:, 0], fw.at[:, 2], halo_send.at[1], halo_recv.at[2], down)
     start_down(f_down)
 
     def cleared(ref):
@@ -286,7 +302,7 @@
     def _():
         cleared(m.at[0, body_rows])
         for c in range(3):
-            cleared(y0h.at[c, 0])
+            cleared(y0h.at[c])
 
     @pl.when(s == spaces - 1)
     def _():
@@ -308,30 +324,36 @@
             for copy in copies:
                 copy.wait_recv()
 
-    def modes(plane, row, n):
-        return [plane_modes(ref[pl.ds(row, n), :], ref[pl.ds(row + 1, n), :]) for ref in plane]
-
-    y0_planes = [
-        [y0h.at[c, 0] for c in range(3)],
-        [y0.at[c, 0] for c in range(3)],
-        [y0.at[c, 1] for c in range(3)],
-        [y0h.at[c, 1] for c in range(3)],
-    ]
-    y1_planes = [
-        [y1.at[c, 0] for c in range(3)],
-        [y1.at[c, 1] for c in range(3)],
-        [y1h.at[c] for c in range(3)],
-    ]
+    def along_x(value, out, at):
+        after = shifted_down(value)
+        out[0, at, :] = value + after
+        out[1, at, :] = after - value
+
+    def plane_along_x(planes, n):
+        def body(row):
+            at = pl.ds(row, n)
+            for source, out in planes:
+                for c in range(3):
+                    along_x(source(c, at), out.at[c], at)
+
+        over_rows(body, n)
+
+    pairs = lambda ref: [(ref.at[c, 0], ref.at[c, 1]) for c in range(3)]
+    y0_planes = [pairs(y0x.at[plane]) for plane in range(4)]
+    y1_planes = [pairs(y1x.at[plane]) for plane in range(3)]
+    fw_planes = [pairs(fwx.at[plane]) for plane in range(3)]
 
     def forward_stress(layer, n):
         def body(row):
-            low = modes([fw.at[c, layer] for c in range(3)], row, n)
-            high = modes([fw.at[c, layer + 1] for c in range(3)], row, n)
+            low = plane_modes(fw_planes[layer], row, n)
+            high = plane_modes(fw_planes[layer + 1], row, n)
             for i, value in enumerate(stresses(strains(low, high))):
                 ff[layer, i, pl.ds(row, n), :] = value
 
         over_rows(body, n)
 
+    plane_along_x([(lambda c, at: y0[c, 1, at, :], y0x.at[2])], 32)
+    plane_along_x([(lambda c, at, k=k: fw[c, k, at, :], fwx.at[k]) for k in range(2)], 32)
     forward_stress(0, 32)
 
     wait_from_below(m_up)
@@ -339,82 +361,80 @@
     pl.semaphore_wait(known1, len(next1))
     tell(known2, next2)
 
-    def own_second(row, n=CHUNK):
+    def own_second(row, n):
         at = pl.ds(row, n)
         inverse = (1 - msk[0, at, :]).astype(F32) * inverse_diagonal(0, 1, row, n)
         inv[0, at, :] = inverse
         beyond = inverse_diagonal(2, 3, row, n)
         for c in range(3):
-            y0[c, 0, at, :] = inverse * r0[c, 0, at, :]
-            y0h[c, 1, at, :] = beyond * r0h[c, at, :]
-
-    def product(row, held, n=16):
-        carried, norm, curve, next_norm = held
+            field = inverse * r0[c, 0, at, :]
+            y0[c, 0, at, :] = field
+            along_x(y0h[c, at, :], y0x.at[0, c], at)
+            along_x(field, y0x.at[1, c], at)
+            along_x(beyond * r0h[c, at, :], y0x.at[3, c], at)
+
+    def product(row, next_norm, n=STEP):
         at = pl.ds(row, n)
-        row_first = lax.broadcasted_iota(jnp.int32, (TILE, ROWS), 0) == 0
-        planes = [modes(plane, row, n) for plane in y0_planes]
-        onto = [None, None]
+        planes = [plane_modes(plane, row, n) for plane in y0_planes]
+        layers = []
         for layer in range(3):
-            modulus = UNIT * m[layer, pl.ds(row + TILE, n), :]
-            force = corner_modes([modulus * f for f in stresses(strains(planes[layer], planes[layer + 1]))])
-            for plane, spread in ((layer - 1, onto_lower), (layer, onto_upper)):
-                if 0 <= plane < 2:
-                    new = [spread(g) for g in force]
-                    if onto[plane] is None:
-                        onto[plane] = new
-                    else:
-                        onto[plane] = [tuple(a + b for a, b in zip(o, w)) for o, w in zip(onto[plane], new)]
-        passed = []
+            modulus = m[layer, pl.ds(row + TILE, n), :]
+            layers.append(corner_modes(stresses(strains(planes[layer], planes[layer + 1]), modulus)))
         for plane in range(2):
             inverse = inv[plane, at, :]
             for c in range(3):
-                g = onto[plane][c]
+                g = onto_plane(layers[plane][c], layers[plane + 1][c])
                 sums = (g[0] - g[1]) + shifted_up(g[0] + g[1])
                 slopes = (g[2] - g[3]) + shifted_up(g[2] + g[3])
-                rolled = pltpu.roll(sums + slopes, 1, 0)
-                head = jnp.where(row_first, carried[3 * plane + c], rolled[0:TILE])
-                passed.append(rolled[0:TILE])
-                if n > TILE:
-                    head = jnp.concatenate([head, rolled[TILE:n]], axis=0)
-                force = (sums - slopes) + head
+                passed[3 * plane + c, pl.ds(row + TILE, n), :] = sums + slopes
+                force = (sums - slopes) + passed[3 * plane + c, pl.ds(row + TILE - 1, n), :]
                 image = inverse * force
                 y1[c, plane, at, :] = image
-                field = y0[c, plane, at, :]
-                norm = norm + folded(r0[c, plane, at, :] * field)
-                curve = curve + folded(force * field)
                 next_norm = next_norm + folded(force * image)
-        return tuple(passed), norm, curve, next_norm
-
-    held = ((zero,) * 6, zero, zero, zero)
+        return next_norm
+
+    next_norm = zero
     for i in range(CHUNKS):
         wait_from_above(r_down[i])
         wait_from_below(y_up[i])
-        over_rows(own_second, CHUNK, None, i * CHUNK, (i + 1) * CHUNK)
-        held = over_rows(product, STEP, held, DONE[i], DONE[i + 1])
+        own_second(CUTS[i], CUTS[i + 1] - CUTS[i])
+        next_norm = over_rows(product, STEP, next_norm, DONE[i], DONE[i + 1])
         start_down(y1_down[i])
-    _, norm, curve, next_norm = held
     pl.semaphore_wait(known2, len(next2))
     tell(known3, next3)
 
     def against_forward(planes, out, n):
         def body(row):
-            all_modes = [modes(plane, row, n) for plane in planes]
+            all_modes = [plane_modes(plane, row, n) for plane in planes]
             at = pl.ds(row, n)
             for layer in range(2):
                 e = strains(all_modes[layer], all_modes[layer + 1])
-                out[layer, at, :] = UNIT * dot(e, [ff[layer, j, at, :] for j in range(18)])
+                out[layer, at, :] = dot(e, [ff[layer, j, at, :] for j in range(18)])
 
         over_rows(body, n)
 
     def energy_of(layer, n):
         def body(row, held):
-            e = strains(modes(y1_planes[layer], row, n), modes(y1_planes[layer + 1], row, n))
-            return held + folded((UNIT * m[1 + layer, pl.ds(row + TILE, n), :]) * dot(e, stresses(e)))
+            e = strains(plane_modes(y1_planes[layer], row, n), plane_modes(y1_planes[layer + 1], row, n))
+            return held + folded(m[1 + layer, pl.ds(row + TILE, n), :] * dot(e, stresses(e)))
 
         return body
 
+    def against_rhs(row, held, n=32):
+        norm, curve = held
+        at = pl.ds(row, n)
+        for c in range(3):
+            for plane in range(2):
+                residual = r0[c, plane, at, :]
+                norm = norm + folded(residual * y0[c, plane, at, :])
+                curve = curve + folded(residual * y1[c, plane, at, :])
+        return norm, curve
+
+    plane_along_x([(lambda c, at, k=k: y1[c, k, at, :], y1x.at[k]) for k in range(2)], 32)
     energy = over_rows(energy_of(0, 32), 32, zero)
+    norm, curve = over_rows(against_rhs, 32, (zero, zero))
     wait_from_above(f_down)
+    plane_along_x([(lambda c, at: fw[c, 2, at, :], fwx.at[2])], 32)
     forward_stress(1, 32)
     against_forward(y0_planes[1:4], g0, 16)
 
@@ -431,6 +451,9 @@
     exchange(g0, 0)
     for i in range(CHUNKS):
         wait_from_above(y1_down[i])
+        part_rows = pl.ds(DONE[i], DONE[i + 1] - DONE[i])
+        for c in range(3):
+            along_x(y1h[c, part_rows, :], y1x.at[2, c], part_rows)
         first, last = DONE[i] - STEP, DONE[i + 1] - STEP
         energy = over_rows(energy_of(1, STEP), STEP, energy, max(first, 0), ROWS if i == CHUNKS - 1 else last)
 
@@ -454,10 +477,10 @@
         total = total + r1[i]
     mid[...] = total
     pl.semaphore_wait(known3, len(next3))
+    for peer in peers_other:
+        remote(mid, r2.at[outer, load], sum_send.at[3], sum_recv.at[3], peer).start()
     for peer in peers_own:
         remote(mid, r2.at[outer, load], sum_send.at[2], sum_recv.at[2], peer).start()
-    for peer in peers_other:
-        remote(mid, r2.at[outer, load], sum_send.at[3], sum_recv.at[3], peer).start()
     r2[outer, load] = total
 
     def coefficients(sums):
@@ -555,8 +578,9 @@
             out_specs=(anywhere,) * 2,
             scratch_shapes=[
                 vmem(3, 2, *plane), vmem(2, rows, ROWS), pltpu.SMEM(zone_base.shape, F32),
-                vmem(2, *plane), ints(2, *plane), ints(2, *plane), vmem(3, 2, *plane), vmem(3, 3, *padded),
-                vmem(2, *plane), vmem(4, *padded), vmem(3, 2, *padded), vmem(3, 2, *padded), vmem(3, 2, *padded), vmem(3, *padded),
+                vmem(2, *plane), ints(2, *plane), ints(2, *plane), vmem(3, 2, *plane), vmem(3, 3, *plane),
+                vmem(2, *plane), vmem(4, *padded), vmem(3, 2, *plane), vmem(3, 2, *plane), vmem(3, *plane), vmem(3, *plane),
+                vmem(4, 3, 2, *padded), vmem(3, 3, 2, *padded), vmem(3, 3, 2, *padded), vmem(6, *padded),
                 vmem(2, *plane), vmem(3, 2, *plane), vmem(3, *plane), vmem(2, 18, *plane),
                 vmem(2, *plane), vmem(2, *plane), vmem(2 * loads, 2, rows, ROWS),
                 vmem(1, ROWS), vmem(group, 1, ROWS), vmem(1, ROWS), vmem(spaces // group, loads, 1, ROWS),

time: 35.3 us -> 34.1 us (0.966)
  Pallas kernels: 34.5 us -> 33.4 us
    pallas_call x1, Pallas kernels: 33.7 us -> 32.6 us  [shards(): pl.pallas_call(functools.partial(kernel, spaces=spaces, loads=loads, grou...]
where the time goes in v5:
time: 34.1 us; the launch traced here: 34 us
  Pallas kernels  33.4 us (98%)
  between operations  0.64 us (2%)
    pallas_call x1, Pallas kernels, shards(): pl.pallas_call(functools.partial(kernel, spaces=spaces, loads=loads, grou...  32.6 us
    pallas_call x1, Pallas kernels, shards(): pl.pallas_call(finish, out_shape=(out(1, 3, 2, *plane), out(2, rows, ROWS...  0.77 us

profile of v5, /device:TPU:1, one launch (start us, length us, event | category | flops | bytes accessed | tf_op | source)
XLA Modules:
  0.0 34.0 jit_solution(13335520631543786614)
XLA Ops:
  0.6 32.6 %shard_map.77 = (f32[3,2,128,128]{3,2,1,0:T(8,128)S(1)}, f32[2,16,128]{2,1,0:T(8,128)S(1)}) custom-call(f32[1,3,2,128,128]{4,3,2,1,0:T(8,128)} %fwd_hbm.1, f32[1,3,2,128,128]{4,3,2,1,0:T(8,128)} %rhs_hbm.1, f32[2,128,128]{2,1,0:T(8,128)} %fac_hbm.1, f32[8]{0:T(128)} %base_hbm.1, s32[2,128,128]{2,1,0:T(8,128)} %ids_hbm.1, s32[2,128,128]{2,1,0:T(8,128)} %msk_hbm.1), custom_call_target="tpu_custom_call" | custom-call | tf_op jit(solution)/shard_map/pallas_call | solution.py:574
  33.2 0.8 %shard_map.78 = (f32[1,3,2,128,128]{4,3,2,1,0:T(8,128)}, f32[2,16,128]{2,1,0:T(8,128)}) custom-call(f32[3,2,128,128]{3,2,1,0:T(8,128)S(1)} %get-tuple-element.4.x, f32[2,16,128]{2,1,0:T(8,128)S(1)} %get-tuple-element.5.grad), custom_call_target="tpu_custom_call" | custom-call | tf_op jit(solution)/shard_map/pallas_call | solution.py:593

commit v6 on v5

--- a/solution.py
+++ b/solution.py
@@ -16,6 +16,7 @@
 STEP = 16
 CUTS = [0, 32, 64, 96, 112, ROWS]
 CHUNKS = len(CUTS) - 1
+EARLY = 72
 DONE = [0] + [cut - STEP for cut in CUTS[1:-1]] + [ROWS]
 LIMIT = 40 * 2**20
 
@@ -130,7 +131,7 @@
 def kernel(
     fwd_hbm, rhs_hbm, fac_hbm, base_hbm, ids_hbm, msk_hbm,
     x_hbm, grad_hbm,
-    x_out, grad_out, base, fac, ids, msk, rhs, fw, sc, m, y0, y1, y0h, y1h, y0x, y1x, fwx, passed, inv, r0, r0h, ff, g0, g1, gr,
+    x_out, grad_out, base, fac, ids, msk, rhs, fw, sc, m, y0, y1, y0h, y1h, y0x, y1x, fwx, passed, inv, beyond, r0, r0h, ff, g0, g1, gr,
     part, r1, mid, r2, coefs,
     load_sem, halo_send, halo_recv, sum_send, sum_recv, known1, known2, known3,
     *, spaces, loads, group,
@@ -182,7 +183,7 @@
     stage1 = [lax.rem(within + i, group) for i in order1]
     peers1 = [{"space": outer * group + i} for i in stage1]
     stage2 = [lax.rem(outer + i, wide) * group + within for i in range(wide)]
-    peers_own = [{"space": i} for i in stage2[1:]]
+    peers_own = [{"space": stage2[i]} for i in sorted(range(1, wide), key=lambda i: -far(i, wide))]
     peers_other = [{"space": stage2[i], "load": lax.rem(load + j, loads)} for i, j in order2]
     stage3 = [lax.rem(load + i, loads) for i in sorted(range(1, loads), key=lambda i: -far(i, loads))]
     peers3 = [{"load": i} for i in stage3]
@@ -289,8 +290,11 @@
     start_down(*r_down)
     start_up(*y_up)
     loaded[5].wait()
-    f_down = remote(fw.at[:, 0], fw.at[:, 2], halo_send.at[1], halo_recv.at[2], down)
-    start_down(f_down)
+    f_down = [
+        remote(fw.at[:, 0, part_rows], fw.at[:, 2, part_rows], halo_send.at[1], halo_recv.at[sem], down)
+        for part_rows, sem in ((pl.ds(0, EARLY), 2), (pl.ds(EARLY, ROWS - EARLY), 3 + 3 * CHUNKS))
+    ]
+    start_down(f_down[0])
 
     def cleared(ref):
         def body(row):
@@ -343,14 +347,14 @@
     y1_planes = [pairs(y1x.at[plane]) for plane in range(3)]
     fw_planes = [pairs(fwx.at[plane]) for plane in range(3)]
 
-    def forward_stress(layer, n):
+    def forward_stress(layer, n, start=0, stop=ROWS):
         def body(row):
             low = plane_modes(fw_planes[layer], row, n)
             high = plane_modes(fw_planes[layer + 1], row, n)
             for i, value in enumerate(stresses(strains(low, high))):
                 ff[layer, i, pl.ds(row, n), :] = value
 
-        over_rows(body, n)
+        over_rows(body, n, None, start, stop)
 
     plane_along_x([(lambda c, at: y0[c, 1, at, :], y0x.at[2])], 32)
     plane_along_x([(lambda c, at, k=k: fw[c, k, at, :], fwx.at[k]) for k in range(2)], 32)
@@ -361,17 +365,24 @@
     pl.semaphore_wait(known1, len(next1))
     tell(known2, next2)
 
-    def own_second(row, n):
+    def own_second(row, n=ROWS):
         at = pl.ds(row, n)
         inverse = (1 - msk[0, at, :]).astype(F32) * inverse_diagonal(0, 1, row, n)
         inv[0, at, :] = inverse
-        beyond = inverse_diagonal(2, 3, row, n)
+        beyond[at, :] = inverse_diagonal(2, 3, row, n)
         for c in range(3):
             field = inverse * r0[c, 0, at, :]
             y0[c, 0, at, :] = field
+            along_x(field, y0x.at[1, c], at)
+
+    over_rows(own_second, ROWS)
+
+    def halo(row, n):
+        at = pl.ds(row, n)
+        inverse = beyond[at, :]
+        for c in range(3):
             along_x(y0h[c, at, :], y0x.at[0, c], at)
-            along_x(field, y0x.at[1, c], at)
-            along_x(beyond * r0h[c, at, :], y0x.at[3, c], at)
+            along_x(inverse * r0h[c, at, :], y0x.at[3, c], at)
 
     def product(row, next_norm, n=STEP):
         at = pl.ds(row, n)
@@ -397,13 +408,14 @@
     for i in range(CHUNKS):
         wait_from_above(r_down[i])
         wait_from_below(y_up[i])
-        own_second(CUTS[i], CUTS[i + 1] - CUTS[i])
+        halo(CUTS[i], CUTS[i + 1] - CUTS[i])
         next_norm = over_rows(product, STEP, next_norm, DONE[i], DONE[i + 1])
         start_down(y1_down[i])
+    start_down(f_down[1])
     pl.semaphore_wait(known2, len(next2))
     tell(known3, next3)
 
-    def against_forward(planes, out, n):
+    def against_forward(planes, out, n, start=0, stop=ROWS):
         def body(row):
             all_modes = [plane_modes(plane, row, n) for plane in planes]
             at = pl.ds(row, n)
@@ -411,7 +423,7 @@
                 e = strains(all_modes[layer], all_modes[layer + 1])
                 out[layer, at, :] = dot(e, [ff[layer, j, at, :] for j in range(18)])
 
-        over_rows(body, n)
+        over_rows(body, n, None, start, stop)
 
     def energy_of(layer, n):
         def body(row, held):
@@ -433,22 +445,34 @@
     plane_along_x([(lambda c, at, k=k: y1[c, k, at, :], y1x.at[k]) for k in range(2)], 32)
     energy = over_rows(energy_of(0, 32), 32, zero)
     norm, curve = over_rows(against_rhs, 32, (zero, zero))
-    wait_from_above(f_down)
-    plane_along_x([(lambda c, at: fw[c, 2, at, :], fwx.at[2])], 32)
-    forward_stress(1, 32)
-    against_forward(y0_planes[1:4], g0, 16)
+    def forward_halo(start, stop):
+        at = pl.ds(start, stop - start)
+        for c in range(3):
+            along_x(fw[c, 2, at, :], fwx.at[2, c], at)
+
+    half = ROWS // 2
+    wait_from_above(f_down[0])
+    forward_halo(0, EARLY)
+    forward_stress(1, 32, 0, half)
+    against_forward(y0_planes[1:4], g0, 16, 0, half)
 
     def taken(sem, ref):
         pltpu.make_async_copy(ref, ref, sem).wait()
 
-    def exchange(src, slots):
+    def exchange(src, slots, chosen=None):
         for slot, peer in zip(stage3, peers3):
-            remote(
+            copy = remote(
                 src.at[:, pl.ds(pl.multiple_of(slot * rows, rows), rows)], gr.at[slots + load],
                 sum_send.at[0], sum_recv.at[0], peer,
-            ).start()
-
-    exchange(g0, 0)
+            )
+            if chosen is None:
+                copy.start()
+            else:
+                pl.when(chosen(slot))(copy.start)
+
+    exchange(g0, 0, lambda slot: slot < loads // 2)
+    summed_up = lambda value: jnp.sum(jnp.sum(value, axis=0, keepdims=True), axis=1, keepdims=True)
+    sums = [summed_up(value) for value in (norm, curve, next_norm)]
     for i in range(CHUNKS):
         wait_from_above(y1_down[i])
         part_rows = pl.ds(DONE[i], DONE[i + 1] - DONE[i])
@@ -459,15 +483,20 @@
 
     lane = lax.broadcasted_iota(jnp.int32, (1, ROWS), 1)
     quarter = ROWS // 4
-    sums = [jnp.sum(jnp.sum(v, axis=0, keepdims=True), axis=1, keepdims=True) for v in (norm, curve, next_norm, energy)]
+    last = summed_up(energy)
     part[...] = jnp.where(
         lane < 2 * quarter,
         jnp.where(lane < quarter, sums[0], sums[1]),
-        jnp.where(lane < 3 * quarter, sums[2], sums[3]),
+        jnp.where(lane < 3 * quarter, sums[2], last),
     )
     for peer in peers1:
         remote(part, r1.at[within], sum_send.at[1], sum_recv.at[1], peer).start()
     r1[within] = part[...]
+    wait_from_above(f_down[1])
+    forward_halo(EARLY, ROWS)
+    forward_stress(1, 32, half, ROWS)
+    against_forward(y0_planes[1:4], g0, 16, half, ROWS)
+    exchange(g0, 0, lambda slot: slot >= loads // 2)
     against_forward(y1_planes, g1, 16)
     exchange(g1, loads)
 
@@ -477,10 +506,10 @@
         total = total + r1[i]
     mid[...] = total
     pl.semaphore_wait(known3, len(next3))
+    for peer in peers_own:
+        remote(mid, r2.at[outer, load], sum_send.at[2], sum_recv.at[2], peer).start()
     for peer in peers_other:
         remote(mid, r2.at[outer, load], sum_send.at[3], sum_recv.at[3], peer).start()
-    for peer in peers_own:
-        remote(mid, r2.at[outer, load], sum_send.at[2], sum_recv.at[2], peer).start()
     r2[outer, load] = total
 
     def coefficients(sums):
@@ -501,13 +530,13 @@
     taken(sum_recv.at[2], r2.at[pl.ds(0, wide - 1), 0])
     first, second = coefficients(summed(load))
 
-    def solve(row, n=32):
+    def solve(row, n=ROWS):
         at = pl.ds(row, n)
         for c in range(3):
             for plane in range(2):
                 x_out[c, plane, at, :] = first * y0[c, plane, at, :] + second * y1[c, plane, at, :]
 
-    over_rows(solve, 32)
+    over_rows(solve, ROWS)
     x_copy = pltpu.make_async_copy(x_out, x_hbm, load_sem.at[0])
     x_copy.start()
 
@@ -581,11 +610,11 @@
                 vmem(2, *plane), ints(2, *plane), ints(2, *plane), vmem(3, 2, *plane), vmem(3, 3, *plane),
                 vmem(2, *plane), vmem(4, *padded), vmem(3, 2, *plane), vmem(3, 2, *plane), vmem(3, *plane), vmem(3, *plane),
                 vmem(4, 3, 2, *padded), vmem(3, 3, 2, *padded), vmem(3, 3, 2, *padded), vmem(6, *padded),
-                vmem(2, *plane), vmem(3, 2, *plane), vmem(3, *plane), vmem(2, 18, *plane),
+                vmem(2, *plane), vmem(*plane), vmem(3, 2, *plane), vmem(3, *plane), vmem(2, 18, *plane),
                 vmem(2, *plane), vmem(2, *plane), vmem(2 * loads, 2, rows, ROWS),
                 vmem(1, ROWS), vmem(group, 1, ROWS), vmem(1, ROWS), vmem(spaces // group, loads, 1, ROWS),
                 vmem(2, loads, ROWS),
-                dma((6,)), dma((2,)), dma((3 + 3 * CHUNKS,)), dma((4,)), dma((4,)),
+                dma((6,)), dma((2,)), dma((4 + 3 * CHUNKS,)), dma((4,)), dma((4,)),
                 *[pltpu.SemaphoreType.REGULAR] * 3,
             ],
             compiler_params=pltpu.CompilerParams(collective_id=0, has_side_effects=True, vmem_limit_bytes=LIMIT),

time: 34.1 us -> 33.9 us (level)
  no operation moved by 1% of the time
where the time goes in v6:
time: 33.9 us; the launch traced here: 33.7 us
  Pallas kernels  33.1 us (98%)
  between operations  0.64 us (2%)
    pallas_call x1, Pallas kernels, shards(): pl.pallas_call(functools.partial(kernel, spaces=spaces, loads=loads, grou...  32.3 us
    pallas_call x1, Pallas kernels, shards(): pl.pallas_call(finish, out_shape=(out(1, 3, 2, *plane), out(2, rows, ROWS...  0.77 us

profile of v6, /device:TPU:1, one launch (start us, length us, event | category | flops | bytes accessed | tf_op | source)
XLA Modules:
  0.0 33.7 jit_solution(8492554608088220713)
XLA Ops:
  0.6 32.3 %shard_map.77 = (f32[3,2,128,128]{3,2,1,0:T(8,128)S(1)}, f32[2,16,128]{2,1,0:T(8,128)S(1)}) custom-call(f32[1,3,2,128,128]{4,3,2,1,0:T(8,128)} %fwd_hbm.1, f32[1,3,2,128,128]{4,3,2,1,0:T(8,128)} %rhs_hbm.1, f32[2,128,128]{2,1,0:T(8,128)} %fac_hbm.1, f32[8]{0:T(128)} %base_hbm.1, s32[2,128,128]{2,1,0:T(8,128)} %ids_hbm.1, s32[2,128,128]{2,1,0:T(8,128)} %msk_hbm.1), custom_call_target="tpu_custom_call" | custom-call | tf_op jit(solution)/shard_map/pallas_call | solution.py:603
  32.9 0.8 %shard_map.78 = (f32[1,3,2,128,128]{4,3,2,1,0:T(8,128)}, f32[2,16,128]{2,1,0:T(8,128)}) custom-call(f32[3,2,128,128]{3,2,1,0:T(8,128)S(1)} %get-tuple-element.4.x, f32[2,16,128]{2,1,0:T(8,128)S(1)} %get-tuple-element.5.grad), custom_call_target="tpu_custom_call" | custom-call | tf_op jit(solution)/shard_map/pallas_call | solution.py:622

commit v7 on v6

--- a/solution.py
+++ b/solution.py
@@ -17,7 +17,8 @@
 CUTS = [0, 32, 64, 96, 112, ROWS]
 CHUNKS = len(CUTS) - 1
 EARLY = 72
-DONE = [0] + [cut - STEP for cut in CUTS[1:-1]] + [ROWS]
+DONE = [0] + [cut - STEP for cut in CUTS[1:]] + [ROWS]
+PIECES = len(DONE) - 1
 LIMIT = 40 * 2**20
 
 POISSON = 0.3
@@ -146,15 +147,10 @@
     def local(src, dst, index):
         return pltpu.make_async_copy(src, dst, load_sem.at[index])
 
-    loaded = [
-        local(base_hbm, base, 5),
-        local(fac_hbm, fac, 0),
-        local(ids_hbm, ids, 1),
-        local(msk_hbm, msk, 2),
-        local(rhs_hbm.at[0], rhs, 3),
-        local(fwd_hbm.at[0], fw.at[:, pl.ds(0, 2)], 4),
-    ]
-    for copy in loaded:
+    zones = [local(base_hbm, base, 5)]
+    zones += [local(fac_hbm.at[k], fac.at[k], k) for k in range(2)] + [local(ids_hbm.at[k], ids.at[k], 2 + k) for k in range(2)]
+    loaded = [local(msk_hbm, msk, 6), local(rhs_hbm.at[0], rhs, 7), local(fwd_hbm.at[0], fw.at[:, pl.ds(0, 2)], 4)]
+    for copy in zones + loaded:
         copy.start()
 
     core, y = lax.rem(s, 2), lax.rem(s // 2, LONG)
@@ -206,7 +202,7 @@
             for plane in range(4):
                 y0x[plane, c, k, past, :] = zero
 
-    for copy in loaded[:3]:
+    for copy in zones:
         copy.wait()
     bases = [base[i] for i in range(base.shape[0])]
 
@@ -245,8 +241,8 @@
     start_down(m_down)
     tell(known1, next1)
 
-    loaded[3].wait()
-    loaded[4].wait()
+    loaded[0].wait()
+    loaded[1].wait()
 
     def inverse_diagonal(low, high, row, n):
         here = m[low, pl.ds(row + TILE, n), :] + m[high, pl.ds(row + TILE, n), :]
@@ -280,19 +276,20 @@
                 halo_send.at[0], halo_recv.at[3 + CHUNKS + i], up,
             )
         )
+    for i in range(PIECES):
         done = pl.ds(DONE[i], DONE[i + 1] - DONE[i])
         y1_down.append(
             remote(
                 y1.at[:, 0, done], y1h.at[:, done],
-                halo_send.at[1], halo_recv.at[3 + 2 * CHUNKS + i], down,
+                halo_send.at[1], halo_recv.at[4 + 2 * CHUNKS + i], down,
             )
         )
     start_down(*r_down)
     start_up(*y_up)
-    loaded[5].wait()
+    loaded[2].wait()
     f_down = [
         remote(fw.at[:, 0, part_rows], fw.at[:, 2, part_rows], halo_send.at[1], halo_recv.at[sem], down)
-        for part_rows, sem in ((pl.ds(0, EARLY), 2), (pl.ds(EARLY, ROWS - EARLY), 3 + 3 * CHUNKS))
+        for part_rows, sem in ((pl.ds(0, EARLY), 2), (pl.ds(EARLY, ROWS - EARLY), 3 + 2 * CHUNKS))
     ]
     start_down(f_down[0])
 
@@ -409,8 +406,9 @@
         wait_from_above(r_down[i])
         wait_from_below(y_up[i])
         halo(CUTS[i], CUTS[i + 1] - CUTS[i])
-        next_norm = over_rows(product, STEP, next_norm, DONE[i], DONE[i + 1])
-        start_down(y1_down[i])
+        for piece in range(i, PIECES if i == CHUNKS - 1 else i + 1):
+            next_norm = over_rows(product, STEP, next_norm, DONE[piece], DONE[piece + 1])
+            start_down(y1_down[piece])
     start_down(f_down[1])
     pl.semaphore_wait(known2, len(next2))
     tell(known3, next3)
@@ -473,13 +471,13 @@
     exchange(g0, 0, lambda slot: slot < loads // 2)
     summed_up = lambda value: jnp.sum(jnp.sum(value, axis=0, keepdims=True), axis=1, keepdims=True)
     sums = [summed_up(value) for value in (norm, curve, next_norm)]
-    for i in range(CHUNKS):
+    for i in range(PIECES):
         wait_from_above(y1_down[i])
         part_rows = pl.ds(DONE[i], DONE[i + 1] - DONE[i])
         for c in range(3):
             along_x(y1h[c, part_rows, :], y1x.at[2, c], part_rows)
         first, last = DONE[i] - STEP, DONE[i + 1] - STEP
-        energy = over_rows(energy_of(1, STEP), STEP, energy, max(first, 0), ROWS if i == CHUNKS - 1 else last)
+        energy = over_rows(energy_of(1, STEP), STEP, energy, max(first, 0), ROWS if i == PIECES - 1 else last)
 
     lane = lax.broadcasted_iota(jnp.int32, (1, ROWS), 1)
     quarter = ROWS // 4
@@ -557,7 +555,9 @@
         taken(halo_send.at[1], ff.at[0, pl.ds(0, 10)])
 
     taken(sum_recv.at[3], r2.at[pl.ds(0, wide), pl.ds(0, loads - 1)])
-    first, second = coefficients(jnp.concatenate([summed(j) for j in range(loads)], axis=0))
+    for j in range(loads):
+        coefs[0, j : j + 1, :] = summed(j)
+    first, second = coefficients(coefs[0])
     coefs[0] = jnp.broadcast_to(first, (loads, ROWS))
     coefs[1] = jnp.broadcast_to(second, (loads, ROWS))
     total = None
@@ -614,7 +614,7 @@
                 vmem(2, *plane), vmem(2, *plane), vmem(2 * loads, 2, rows, ROWS),
                 vmem(1, ROWS), vmem(group, 1, ROWS), vmem(1, ROWS), vmem(spaces // group, loads, 1, ROWS),
                 vmem(2, loads, ROWS),
-                dma((6,)), dma((2,)), dma((4 + 3 * CHUNKS,)), dma((4,)), dma((4,)),
+                dma((8,)), dma((2,)), dma((4 + 2 * CHUNKS + PIECES,)), dma((4,)), dma((4,)),
                 *[pltpu.SemaphoreType.REGULAR] * 3,
             ],
             compiler_params=pltpu.CompilerParams(collective_id=0, has_side_effects=True, vmem_limit_bytes=LIMIT),

time: 33.9 us -> 33.8 us (level)
  no operation moved by 1% of the time
where the time goes in v7:
time: 33.8 us; the launch traced here: 33.7 us
  Pallas kernels  33.1 us (98%)
  between operations  0.64 us (2%)
    pallas_call x1, Pallas kernels, shards(): pl.pallas_call(functools.partial(kernel, spaces=spaces, loads=loads, grou...  32.3 us
    pallas_call x1, Pallas kernels, shards(): pl.pallas_call(finish, out_shape=(out(1, 3, 2, *plane), out(2, rows, ROWS...  0.77 us

profile of v7, /device:TPU:1, one launch (start us, length us, event | category | flops | bytes accessed | tf_op | source)
XLA Modules:
  0.0 33.7 jit_solution(11674141729560319754)
XLA Ops:
  0.6 32.3 %shard_map.77 = (f32[3,2,128,128]{3,2,1,0:T(8,128)S(1)}, f32[2,16,128]{2,1,0:T(8,128)S(1)}) custom-call(f32[1,3,2,128,128]{4,3,2,1,0:T(8,128)} %fwd_hbm.1, f32[1,3,2,128,128]{4,3,2,1,0:T(8,128)} %rhs_hbm.1, f32[2,128,128]{2,1,0:T(8,128)} %fac_hbm.1, f32[8]{0:T(128)} %base_hbm.1, s32[2,128,128]{2,1,0:T(8,128)} %ids_hbm.1, s32[2,128,128]{2,1,0:T(8,128)} %msk_hbm.1), custom_call_target="tpu_custom_call" | custom-call | tf_op jit(solution)/shard_map/pallas_call | solution.py:603
  32.9 0.8 %shard_map.78 = (f32[1,3,2,128,128]{4,3,2,1,0:T(8,128)}, f32[2,16,128]{2,1,0:T(8,128)}) custom-call(f32[3,2,128,128]{3,2,1,0:T(8,128)S(1)} %get-tuple-element.4.x, f32[2,16,128]{2,1,0:T(8,128)S(1)} %get-tuple-element.5.grad), custom_call_target="tpu_custom_call" | custom-call | tf_op jit(solution)/shard_map/pallas_call | solution.py:622

commit v8 on v7

--- a/solution.py
+++ b/solution.py
@@ -131,8 +131,8 @@
 
 def kernel(
     fwd_hbm, rhs_hbm, fac_hbm, base_hbm, ids_hbm, msk_hbm,
-    x_hbm, grad_hbm,
-    x_out, grad_out, base, fac, ids, msk, rhs, fw, sc, m, y0, y1, y0h, y1h, y0x, y1x, fwx, passed, inv, beyond, r0, r0h, ff, g0, g1, gr,
+    x_out, grad_out,
+    base, fac, ids, msk, rhs, fw, sc, m, y0, y1, y0h, y1h, y0x, y1x, fwx, passed, inv, beyond, r0, r0h, ff, g0, g1, gr,
     part, r1, mid, r2, coefs,
     load_sem, halo_send, halo_recv, sum_send, sum_recv, known1, known2, known3,
     *, spaces, loads, group,
@@ -535,8 +535,6 @@
                 x_out[c, plane, at, :] = first * y0[c, plane, at, :] + second * y1[c, plane, at, :]
 
     over_rows(solve, ROWS)
-    x_copy = pltpu.make_async_copy(x_out, x_hbm, load_sem.at[0])
-    x_copy.start()
 
     mine = pl.ds(pl.multiple_of(load * rows, rows), rows)
     gr[load] = g0[:, mine, :]
@@ -565,13 +563,9 @@
         term = coefs[0, i : i + 1, :][None] * gr[i] + coefs[1, i : i + 1, :][None] * gr[loads + i]
         total = term if total is None else total + term
     grad_out[...] = sc[:, mine, :] * total
-    grad_copy = pltpu.make_async_copy(grad_out, grad_hbm, load_sem.at[1])
-    grad_copy.start()
 
     taken(sum_send.at[3], r2.at[pl.ds(0, wide), pl.ds(0, loads - 1)])
     taken(sum_send.at[2], r2.at[pl.ds(0, wide - 1), 0])
-    x_copy.wait()
-    grad_copy.wait()
 
 
 def finish(x, grad, x_out, grad_out, sem):
@@ -604,9 +598,9 @@
             functools.partial(kernel, spaces=spaces, loads=loads, group=group),
             out_shape=(out(3, 2, *plane), out(2, rows, ROWS)),
             in_specs=[hbm] * 6,
-            out_specs=(anywhere,) * 2,
+            out_specs=(pl.BlockSpec(memory_space=pltpu.VMEM),) * 2,
             scratch_shapes=[
-                vmem(3, 2, *plane), vmem(2, rows, ROWS), pltpu.SMEM(zone_base.shape, F32),
+                pltpu.SMEM(zone_base.shape, F32),
                 vmem(2, *plane), ints(2, *plane), ints(2, *plane), vmem(3, 2, *plane), vmem(3, 3, *plane),
                 vmem(2, *plane), vmem(4, *padded), vmem(3, 2, *plane), vmem(3, 2, *plane), vmem(3, *plane), vmem(3, *plane),
                 vmem(4, 3, 2, *padded), vmem(3, 3, 2, *padded), vmem(3, 3, 2, *padded), vmem(6, *padded),

time: 33.8 us -> 33.8 us (level)
  no operation moved by 1% of the time
where the time goes in v8:
time: 33.8 us; the launch traced here: 33.7 us
  Pallas kernels  33 us (98%)
  between operations  0.64 us (2%)
    pallas_call x1, Pallas kernels, shards(): pl.pallas_call(functools.partial(kernel, spaces=spaces, loads=loads, grou...  32.3 us
    pallas_call x1, Pallas kernels, shards(): pl.pallas_call(finish, out_shape=(out(1, 3, 2, *plane), out(2, rows, ROWS...  0.77 us

profile of v8, /device:TPU:1, one launch (start us, length us, event | category | flops | bytes accessed | tf_op | source)
XLA Modules:
  0.0 33.7 jit_solution(2313086171749731145)
XLA Ops:
  0.6 32.3 %shard_map.77 = (f32[3,2,128,128]{3,2,1,0:T(8,128)S(1)}, f32[2,16,128]{2,1,0:T(8,128)S(1)}) custom-call(f32[1,3,2,128,128]{4,3,2,1,0:T(8,128)} %fwd_hbm.1, f32[1,3,2,128,128]{4,3,2,1,0:T(8,128)} %rhs_hbm.1, f32[2,128,128]{2,1,0:T(8,128)} %fac_hbm.1, f32[8]{0:T(128)} %base_hbm.1, s32[2,128,128]{2,1,0:T(8,128)} %ids_hbm.1, s32[2,128,128]{2,1,0:T(8,128)} %msk_hbm.1), custom_call_target="tpu_custom_call" | custom-call | tf_op jit(solution)/shard_map/pallas_call | solution.py:597
  32.9 0.8 %shard_map.78 = (f32[1,3,2,128,128]{4,3,2,1,0:T(8,128)}, f32[2,16,128]{2,1,0:T(8,128)}) custom-call(f32[3,2,128,128]{3,2,1,0:T(8,128)S(1)} %get-tuple-element.4.x, f32[2,16,128]{2,1,0:T(8,128)S(1)} %get-tuple-element.5.grad), custom_call_target="tpu_custom_call" | custom-call | tf_op jit(solution)/shard_map/pallas_call | solution.py:616
